TPU v7x, 32 devices: a whole 2x2x4 slice. The times are simulated.
32 devices in a mesh: groups: 2 (over x), gz: 16 (over z, y, core).
Axes of the slice: x: 2, y: 2, z: 4, core: 2. Of those that a mesh axis runs over, the one named last changes fastest.
Arguments:
- estimate: float32 [16, 512, 256], P(None, 'gz', 'groups'), parts along dimension 2, may hold values from 0 to 2
- frames: int32 [3, 5, 16, 512, 256], P(None, None, 'gz', None, 'groups'), parts along dimension 4, may hold values from 0 to 4095
- phase_index: int32 [3, 5], replicated, may hold values from 0 to 4, each once within a row
- axial_otf: float32 [3, 2, 16], replicated, may hold values from -4 to 4
- row_blur: float32 [3, 128, 128], replicated, may hold values from -0.5 to 0.5
- column_taps: float32 [3, 7], replicated, may hold values from 0.1 to 1
Outputs:
- gradient: float32 [16, 512, 256], P(None, 'gz', 'groups'), parts along dimension 2
There are 2 independent parts, one for each index of `groups`. A program takes and returns all parts, laid end to end along the dimension named above; an argument that names none is the same for every part. Nothing has to cross between parts.
Inputs may be any that keep to these rules, and one draw needn't show every extreme that they name: `phase_index`: for each orientation the 5 frames take every phase step once.
All inputs are finite; a program needn't handle non-finite values.
Results may differ from a plain program's by a relative error of at most 0.0001.
Values sent between devices are 32-bit elements; how exact they have to be, the bound alone decides.
No kernel may reach another device: no remote copies, remote signals or barrier semaphores. Data moves between devices by JAX's collectives and lax.ppermute only.
A program may use at most 64 MiB of HBM per device.

v0:
```python
import math

import jax
import jax.numpy as jnp
import numpy as np
from jax import lax
from jax.experimental import pallas as pl
from jax.experimental.pallas import tpu as pltpu
from jax.sharding import PartitionSpec as P


pattern_period = 3.7
orient_base = 0.3
data_scale = 1.0 / 1024.0
PAD = 8


def exact_dot(left_side, right_side):
    return jnp.dot(
        left_side, right_side, preferred_element_type=jnp.float32, precision=lax.Precision.HIGHEST
    )


def split(values):
    high = values.astype(jnp.bfloat16)
    low = (values - high.astype(jnp.float32)).astype(jnp.bfloat16)
    return high, low


def wide(values):
    high, low = split(values)
    return jnp.concatenate([high, low], axis=1)


def weights(matrix):
    row = wide(matrix)
    return jnp.concatenate([row, row], axis=0)


def narrow(product):
    half = product.shape[1] // 2
    return product[:, :half] + product[:, half:]


def wide_dot(left_side, right_side):
    return jnp.dot(left_side, right_side, preferred_element_type=jnp.float32)


def pattern_table(orients, loop_width, row_count):
    columns = np.arange(-PAD, loop_width + PAD) % loop_width
    rows = np.arange(row_count)
    images = []
    for orient in range(orients):
        direction = orient_base + 2.0 * math.pi * orient / 3.0
        phase = (
            columns.astype(np.float32)[:, None] * np.float32(math.cos(direction))
            + rows.astype(np.float32)[None, :] * np.float32(math.sin(direction))
        ) * np.float32(2.0 * math.pi / pattern_period)
        images += [np.cos(phase.astype(np.float64)), np.sin(phase.astype(np.float64))]
    return np.stack(images).astype(np.float32)


def harmonic_of(cos_one, sin_one, harmonic):
    if harmonic == 1:
        return cos_one, sin_one
    return cos_one * cos_one - sin_one * sin_one, 2.0 * (sin_one * cos_one)


def data_kernel(
    phase_ref, taps_ref, frames_hbm, blur_hbm, table_hbm, out_ref,
    raw, mixed, weight, table, blur_rows, sems, side_sems,
):
    orients, phases = frames_hbm.shape[0], frames_hbm.shape[1]
    loop_width = raw.shape[2]
    _, bands, width, _ = out_ref.shape
    reach = (taps_ref.shape[1] - 1) // 2
    copies = []
    for orient in range(orients):
        row = []
        for index in range(phases):
            copy = pltpu.make_async_copy(
                frames_hbm.at[orient, index, 0],
                raw.at[orient, index],
                sems.at[orient, index],
            )
            copy.start()
            row.append(copy)
        copies.append(row)
    blur_copy = pltpu.make_async_copy(blur_hbm, blur_rows, side_sems.at[0])
    blur_copy.start()
    table_copy = pltpu.make_async_copy(table_hbm, table, side_sems.at[1])
    table_copy.start()
    total = bands * 0 + 4 * orients
    c1, c2 = math.cos(2 * math.pi / 5), math.cos(4 * math.pi / 5)
    s1, s2 = math.sin(2 * math.pi / 5), math.sin(4 * math.pi / 5)
    step = max(64, width)
    for orient in range(orients):
        holder = []
        for step_index in range(phases):
            at_step = 0
            for index in range(1, phases):
                at_step = jnp.where(phase_ref[orient, index] == step_index, index, at_step)
            holder.append(at_step)
        for copy in copies[orient]:
            copy.wait()

        def mix(index, carry):
            rows = pl.ds(pl.multiple_of(index * step, step), step)
            at = pl.ds(pl.multiple_of(index * step + PAD, 8), step)
            f0, f1, f2, f3, f4 = [raw[orient, k, rows, :] for k in holder]
            zero = f0.astype(jnp.float32) * data_scale - 2.0
            near = (f1 + f4).astype(jnp.float32) * data_scale - 4.0
            far = (f2 + f3).astype(jnp.float32) * data_scale - 4.0
            near_odd = (f1 - f4).astype(jnp.float32) * data_scale
            far_odd = (f2 - f3).astype(jnp.float32) * data_scale
            mixed[4 * orient, at, :] = zero + c1 * near + c2 * far
            mixed[4 * orient + 1, at, :] = s1 * near_odd + s2 * far_odd
            mixed[4 * orient + 2, at, :] = zero + c2 * near + c1 * far
            mixed[4 * orient + 3, at, :] = s2 * near_odd - s1 * far_odd
            plain = zero + near + far
            if orient:
                plain = plain + mixed[total, at, :]
            mixed[total, at, :] = plain
            return carry

        lax.fori_loop(0, loop_width // step, mix, 0)
    for image in range(total + 1):
        mixed[image, PAD - reach : PAD, :] = mixed[
            image, loop_width + PAD - reach : loop_width + PAD, :
        ]
        mixed[image, loop_width + PAD : loop_width + PAD + reach, :] = mixed[
            image, PAD : PAD + reach, :
        ]
    blur_copy.wait()
    for band in range(bands):
        weight[band] = weights(blur_rows[band])
    table_copy.wait()

    def blur(image, band, begin):
        acc = None
        for offset in range(-reach, reach + 1):
            tap = taps_ref[band, offset + reach] * (1.0 / (orients * phases))
            term = tap * mixed[image, pl.ds(begin + PAD - offset, step), :]
            acc = term if acc is None else acc + term
        return acc

    shares = step // width

    def store(index, band, values):
        for share in range(shares):
            out_ref[index * shares + share, band] = values[share * width : (share + 1) * width]

    def plain_out(index, carry):
        begin = pl.multiple_of(index * step, step)
        store(index, 0, narrow(wide_dot(wide(blur(total, 0, begin)), weight[0])))
        return carry

    lax.fori_loop(0, loop_width // step, plain_out, 0)
    for band in range(1, bands):

        def band_out(index, carry):
            begin = pl.multiple_of(index * step, step)
            at = pl.ds(begin + PAD, step)
            parts = []
            for orient in range(orients):
                for part in range(2):
                    parts.append(wide(blur(4 * orient + 2 * band - 2 + part, band, begin)))
            product = narrow(wide_dot(jnp.concatenate(parts, axis=0), weight[band]))
            acc = None
            for orient in range(orients):
                cos_pattern, sin_pattern = harmonic_of(
                    table[2 * orient, at, :], table[2 * orient + 1, at, :], band
                )
                even = product[2 * orient * step : (2 * orient + 1) * step]
                odd = product[(2 * orient + 1) * step : (2 * orient + 2) * step]
                term = cos_pattern * even - sin_pattern * odd
                acc = term if acc is None else acc + term
            store(index, band, acc)
            return carry

        lax.fori_loop(0, loop_width // step, band_out, 0)


def data_sums(frames, phase_index, row_blur, column_taps, table, chunks):
    orients, phases, _, loop_width, row_count = frames.shape
    bands = row_blur.shape[0]
    width = loop_width // chunks
    smem = pl.BlockSpec(memory_space=pltpu.SMEM)
    vmem = pl.BlockSpec(memory_space=pltpu.VMEM)
    anywhere = pl.BlockSpec(memory_space=pltpu.HBM)
    images = 4 * orients + 1
    return pl.pallas_call(
        data_kernel,
        out_shape=jax.ShapeDtypeStruct((chunks, bands, width, row_count), jnp.float32),
        in_specs=[smem, smem, anywhere, anywhere, anywhere],
        out_specs=vmem,
        scratch_shapes=[
            pltpu.VMEM((orients, phases, loop_width, row_count), jnp.int32),
            pltpu.VMEM((images, loop_width + 2 * PAD, row_count), jnp.float32),
            pltpu.VMEM((bands, 2 * row_count, 2 * row_count), jnp.bfloat16),
            pltpu.VMEM(table.shape, jnp.float32),
            pltpu.VMEM(row_blur.shape, jnp.float32),
            pltpu.SemaphoreType.DMA((orients, phases)),
            pltpu.SemaphoreType.DMA((2,)),
        ],
        cost_estimate=pl.CostEstimate(
            flops=13 * loop_width * 2 * 256 * 256, bytes_accessed=frames.size * 4, transcendentals=0
        ),
        compiler_params=pltpu.CompilerParams(vmem_limit_bytes=63 << 20),
        name="data_sums",
    )(phase_index, column_taps, frames, row_blur, table)


def estimate_kernel(taps_ref, axial_ref, table_ref, blur_ref, out_ref):
    bands, _, planes, _ = axial_ref.shape
    width = out_ref.shape[0]
    orients = table_ref.shape[0] // 2
    reach = (taps_ref.shape[1] - 1) // 2
    span = 2 * reach
    step = 4

    def lags_of(band, scale):
        return [
            scale
            * sum(
                taps_ref[band, d] * taps_ref[band, d + shift]
                for d in range(0, 2 * reach + 1 - shift)
            )
            for shift in range(span + 1)
        ]

    def filtered(columns, lags):
        rows = []
        for i in range(step):
            acc = lags[0] * columns[i + span]
            for shift in range(1, span + 1):
                acc = acc + lags[shift] * (columns[i + span - shift] + columns[i + span + shift])
            rows.append(wide(acc))
        return rows

    def weight_of(band):
        matrix = blur_ref[band]
        return weights(
            lax.dot_general(
                matrix,
                matrix,
                (((0,), (0,)), ((), ())),
                preferred_element_type=jnp.float32,
                precision=lax.Precision.HIGHEST,
            )
        )

    weight = [weight_of(band) for band in range(bands)]
    lags = [lags_of(0, 1.0)] + [lags_of(band, 0.5 / orients) for band in range(1, bands)]

    def chunk(index, carry):
        begin = index * step
        rows = filtered([axial_ref[0, begin + i] for i in range(step + 2 * span)], lags[0])
        product = narrow(wide_dot(jnp.concatenate(rows, axis=0), weight[0]))
        acc = [product[i * planes : (i + 1) * planes] for i in range(step)]
        for band in range(1, bands):
            rows = []
            patterns = []
            for orient in range(orients):
                pairs = [
                    harmonic_of(
                        table_ref[2 * orient, pl.ds(begin + i, 1), :],
                        table_ref[2 * orient + 1, pl.ds(begin + i, 1), :],
                        band,
                    )
                    for i in range(step + 2 * span)
                ]
                for part in range(2):
                    columns = [
                        pairs[i][part] * axial_ref[band, begin + i]
                        for i in range(step + 2 * span)
                    ]
                    rows += filtered(columns, lags[band])
                    patterns.append([pairs[i + span][part] for i in range(step)])
            product = narrow(wide_dot(jnp.concatenate(rows, axis=0), weight[band]))
            for which, pattern in enumerate(patterns):
                for i in range(step):
                    at = (which * step + i) * planes
                    acc[i] = acc[i] + pattern[i] * product[at : at + planes]
        for i in range(step):
            out_ref[begin + i] = acc[i]
        return carry

    lax.fori_loop(0, width // step, chunk, 0)


def estimate_part(axial, table, row_blur, column_taps, width):
    _, _, planes, row_count = axial.shape
    orients = table.shape[0] // 2
    smem = pl.BlockSpec(memory_space=pltpu.SMEM)
    vmem = pl.BlockSpec(memory_space=pltpu.VMEM)
    rows = 2 * orients * width * planes
    return pl.pallas_call(
        estimate_kernel,
        out_shape=jax.ShapeDtypeStruct((width, planes, row_count), jnp.float32),
        in_specs=[smem, vmem, vmem, vmem],
        out_specs=vmem,
        cost_estimate=pl.CostEstimate(
            flops=40 * rows * 2 * 256 * 256, bytes_accessed=axial.size * 4, transcendentals=0
        ),
        compiler_params=pltpu.CompilerParams(vmem_limit_bytes=40 << 20),
        name="estimate_part",
    )(column_taps, axial, table, row_blur)


def combine_kernel(adjoint_ref, estimate_ref, received_ref, out_ref):
    width, planes, _ = estimate_ref.shape
    high, low = split(adjoint_ref[...])
    left_side = jnp.concatenate([high, high, low], axis=1)
    depth = adjoint_ref.shape[1]
    for index in range(width):
        high, low = split(received_ref[pl.ds(index, depth, stride=width), :])
        right_side = jnp.concatenate([high, low, high], axis=0)
        out_ref[pl.ds(index, planes, stride=width), :] = estimate_ref[index] - wide_dot(
            left_side, right_side
        )


def combine(adjoint, from_estimate, received):
    width, planes, row_count = from_estimate.shape
    depth = adjoint.shape[1]
    vmem = pl.BlockSpec(memory_space=pltpu.VMEM)
    return pl.pallas_call(
        combine_kernel,
        out_shape=jax.ShapeDtypeStruct((planes * width, row_count), jnp.float32),
        in_specs=[vmem, vmem, vmem],
        out_specs=vmem,
        cost_estimate=pl.CostEstimate(
            flops=2 * received.size * planes, bytes_accessed=received.size * 4, transcendentals=0
        ),
        compiler_params=pltpu.CompilerParams(vmem_limit_bytes=24 << 20),
        name="combine",
    )(adjoint, from_estimate, received.reshape(depth * width, row_count)).reshape(
        planes, width, row_count
    )


def halo(estimate, span):
    ring = lax.axis_size("gz")
    width = estimate.shape[1]
    lefts, rights = [], []
    hop, missing = 1, span
    while missing > 0:
        take = min(missing, width)
        lefts.insert(
            0,
            lax.ppermute(
                estimate[:, width - take :], "gz", [(s, (s + hop) % ring) for s in range(ring)]
            ),
        )
        rights.append(
            lax.ppermute(estimate[:, :take], "gz", [(s, (s - hop) % ring) for s in range(ring)])
        )
        missing -= take
        hop += 1
    return jnp.concatenate(lefts + [estimate] + rights, axis=1)


def axial_matrices(axial_otf, planes):
    wrapped = np.arange(planes)[:, None] * np.arange(planes)[None, :] % planes
    angle = wrapped * (2.0 * math.pi / planes)
    cosine = np.cos(angle).astype(np.float32)
    sine = np.sin(angle).astype(np.float32)
    real = axial_otf[:, 0, :, None]
    imag = axial_otf[:, 1, :, None]
    inner = jnp.concatenate(
        [real * cosine + imag * sine, real * sine - imag * cosine], axis=1
    )
    both = np.concatenate([cosine, sine], axis=1) / planes
    return jnp.einsum(
        "zk,mkw->mzw", both, inner, precision=lax.Precision.HIGHEST,
        preferred_element_type=jnp.float32,
    )


def shards(estimate, frames, phase_index, axial_otf, row_blur, column_taps):
    planes, width, row_count = estimate.shape
    ring = lax.axis_size("gz")
    orients = frames.shape[0]
    bands = row_blur.shape[0]
    span = column_taps.shape[1] - 1
    table = jnp.asarray(pattern_table(orients, width * ring, row_count))
    sums = data_sums(frames, phase_index, row_blur, column_taps, table, ring)
    estimate, sums = lax.optimization_barrier((estimate, sums))
    extended = halo(estimate, span)
    received = lax.all_to_all(sums, "gz", 0, 0, tiled=True)
    forward = axial_matrices(axial_otf, planes)
    squared = jnp.einsum("mzw,mzv->mwv", forward, forward, precision=lax.Precision.HIGHEST)
    axial = exact_dot(squared.reshape(bands * planes, planes), extended.reshape(planes, -1))
    axial = axial.reshape(bands, planes, width + 2 * span, row_count).transpose(0, 2, 1, 3)
    begin = lax.axis_index("gz") * width + (PAD - span)
    near = lax.dynamic_slice_in_dim(table, begin, width + 2 * span, axis=1)
    from_estimate = estimate_part(axial, near, row_blur, column_taps, width)
    adjoint = forward.transpose(2, 1, 0).reshape(planes, planes * bands)
    return combine(adjoint, from_estimate, received)


def solution(mesh):
    placed = (P(None, "gz", "groups"), P(None, None, "gz", None, "groups"), P(), P(), P(), P())
    return jax.shard_map(
        shards, mesh=mesh, in_specs=placed, out_specs=P(None, "gz", "groups"), check_vma=False
    )
```

profile of v0, /device:TPU:0, one launch (start us, length us, event | category | flops | bytes accessed | tf_op | source)
XLA Modules:
  0.0 41.3 jit_solution(4343993882824277646)
XLA Ops:
  0.0 0.0 copy-start.2
  0.0 9.8 %data_sums.1 = f32[16,3,32,128]{3,2,1,0:T(8,128)} custom-call(s32[3,5]{1,0:T(4,128)} %phase_ref.1, f32[3,7]{1,0:T(4,128)} %taps_ref.3, s32[3,5,1,512,128]{4,3,2,1,0:T(8,128)} %frames_hbm.1, f32[3,128,128]{2,1,0:T(8,128)} %blur_ref.1, f32[6,528,128]{2,1,0:T(8,128)} %constant.21.clone.table_hbm), custom_call_target="tpu_custom_call" | custom-call | flops 872415232 | bytes 3932160 | tf_op jit(solution)/shard_map/data_sums/pallas_call | solution.py:192
  9.9 0.0 copy-done.2
  9.9 0.0 copy-start.6
  9.9 0.0 copy-start.4
  9.9 0.0 copy-start.5
  9.9 0.0 copy-start.3
  9.9 5.5 %collective-permute-start.1 = (f32[16,6,128]{2,1,0:T(8,128)S(1)}, f32[16,6,128]{2,1,0:T(8,128)S(1)}, u32[]{:S(2)}, u32[]{:S(2)}) collective-permute-start(f32[16,6,128]{2,1,0:T(8,128)S(1)} %get-tuple-element.10), channel_id=1, source_target_pairs={{0,15},{1,0},{2,1},{3,2},{4,3},{5,4},{6,5},{7,6},{8,7},{9,8},{10,9... | collective-permute-start | bytes 147464 | tf_op jit(solution)/shard_map/ppermute | solution.py:357
  15.5 0.0 collective-permute-start
  15.5 5.8 %all-to-all-start = ((f32[16,3,32,128]{3,2,1,0:T(8,128)}), f32[16,3,32,128]{3,2,1,0:T(8,128)S(1)}, u32[]{:S(2)}, u32[]{:S(2)}) async-start(f32[16,3,32,128]{3,2,1,0:T(8,128)} %data_sums.1), calls=%async_computation | async-start | bytes 1572864 | tf_op jit(solution)/shard_map/all_to_all | solution.py:391
  21.3 0.0 copy-start
  21.3 0.0 copy-start.1
  21.3 0.0 copy-done.6
  21.4 1.0 %constant_dynamic-slice_fusion.table_ref = f32[6,44,128]{2,1,0:T(8,128)S(1)} fusion(f32[6,528,128]{2,1,0:T(8,128)} %constant.21.clone.table_hbm, s32[]{:T(128)S(6)} %select_n.3), kind=kLoop, calls=%fused_computation.14 | loop fusion | bytes 270340 | tf_op jit(solution)/shard_map/dynamic_slice | solution.py:397
  22.4 0.0 copy-done.4
  22.4 0.0 copy-done.5
  22.4 0.0 copy-done.3
  22.4 0.2 fusion.1
  22.6 0.2 convolution_bitcast_fusion.1
  22.8 0.1 copy.12
  22.9 0.1 copy.14.adjoint_ref
  23.0 0.0 collective-permute-done.1
  23.0 0.0 collective-permute-done
  23.0 0.1 pad_maximum_fusion
  23.0 1.0 %convolution_bitcast_fusion.axial_ref = f32[3,44,16,128]{3,2,1,0:T(8,128)S(1)} fusion(f32[3,16,16,1]{2,1,3,0:T(8,128)S(1)} %convolution_bitcast_fusion.1, f32[2,8,44,128]{3,2,1,0:T(8,128)S(1)} %bitcast.37), kind=kOutput, calls=%fused_computation | convolution fusion | flops 51904512 | bytes 1444864 | tf_op jit(solution)/shard_map/dot_general | solution.py:19
  24.0 0.0 copy-done
  24.0 0.0 copy-done.1
  24.0 5.7 %estimate_part.1.estimate_ref = f32[32,16,128]{2,1,0:T(8,128)S(1)} custom-call(f32[3,7]{1,0:T(4,128)S(1)} %copy-done.1, f32[3,44,16,128]{3,2,1,0:T(8,128)S(1)} %convolution_bitcast_fusion.axial_ref, f32[6,44,128]{2,1,0:T(8,128)S(1)} %constant_dynamic-slice_fusion.table_ref, f32[3,128,128]{2,1,0:T(8,128)S(1)} %copy-done), custom_call_target="tpu_custom_call" | custom-call | flops 16106127360 | bytes 1081344 | tf_op jit(solution)/shard_map/estimate_part/pallas_call | solution.py:298
  29.8 10.2 %all-to-all-done = f32[16,3,32,128]{3,2,1,0:T(8,128)S(1)} async-done(((f32[16,3,32,128]{3,2,1,0:T(8,128)}), f32[16,3,32,128]{3,2,1,0:T(8,128)S(1)}, u32[]{:S(2)}, u32[]{:S(2)}) %all-to-all-start) | async-done | bytes 786464 | tf_op jit(solution)/shard_map/all_to_all | solution.py:391
  40.0 1.4 %combine.1 = f32[512,128]{1,0:T(8,128)} custom-call(f32[16,48]{1,0:T(8,128)S(1)} %copy.14.adjoint_ref, f32[32,16,128]{2,1,0:T(8,128)S(1)} %estimate_part.1.estimate_ref, f32[1536,128]{1,0:T(8,128)S(1)} %bitcast.36), custom_call_target="tpu_custom_call" | custom-call | flops 6291456 | bytes 786432 | tf_op jit(solution)/shard_map/combine/pallas_call | solution.py:328
  (5 shorter events, 0.1 us)
Async XLA Ops:
  0.0 9.9 %copy-start.2 = (f32[16,32,128]{2,1,0:T(8,128)S(1)}, f32[16,32,128]{2,1,0:T(8,128)}, u32[]{:S(2)}) copy-start(f32[16,32,128]{2,1,0:T(8,128)} %param.10) | copy-start | bytes 786436
  9.9 11.5 %copy-start.6 = (f32[3,2,16]{2,1,0:T(2,128)S(1)}, f32[3,2,16]{2,1,0:T(2,128)}, u32[]{:S(2)}) copy-start(f32[3,2,16]{2,1,0:T(2,128)} %param.13) | copy-start | bytes 1156
  9.9 12.5 %copy-start.4 = (f32[16,16]{0,1:T(8,128)S(1)}, f32[16,16]{0,1:T(8,128)}, u32[]{:S(2)}) copy-start(f32[16,16]{0,1:T(8,128)} %constant.23.clone) | copy-start | bytes 3076
  9.9 12.5 %copy-start.5 = (f32[16,16]{0,1:T(8,128)S(1)}, f32[16,16]{0,1:T(8,128)}, u32[]{:S(2)}) copy-start(f32[16,16]{0,1:T(8,128)} %constant.22.clone) | copy-start | bytes 3076
  9.9 12.5 %copy-start.3 = (f32[16,32,1]{1,0,2:T(8,128)S(1)}, f32[16,32,1]{1,0,2:T(8,128)}, u32[]{:S(2)}) copy-start(f32[16,32,1]{1,0,2:T(8,128)} %constant.26) | copy-start | bytes 6148
  9.9 13.0 %collective-permute-start.1 = (f32[16,6,128]{2,1,0:T(8,128)S(1)}, f32[16,6,128]{2,1,0:T(8,128)S(1)}, u32[]{:S(2)}, u32[]{:S(2)}) collective-permute-start(f32[16,6,128]{2,1,0:T(8,128)S(1)} %get-tuple-element.10), channel_id=1, source_target_pairs={{0,15},{1,0},{2,1},{3,2},{4,3},{5,4},{6,5},{7,6},{8,7},{9,8},{10,9... | collective-permute-start | bytes 147464 | tf_op jit(solution)/shard_map/ppermute | solution.py:357
  15.5 7.5 %collective-permute-start = (f32[16,6,128]{2,1,0:T(8,128)S(1)}, f32[16,6,128]{2,1,0:T(8,128)S(1)}, u32[]{:S(2)}, u32[]{:S(2)}) collective-permute-start(f32[16,6,128]{2,1,0:T(8,128)S(1)} %get-tuple-element.9), channel_id=1, source_target_pairs={{0,1},{1,2},{2,3},{3,4},{4,5},{5,6},{6,7},{7,8},{8,9},{9,10},{10,1... | collective-permute-start | bytes 147464 | tf_op jit(solution)/shard_map/ppermute | solution.py:352
  15.5 24.5 %all-to-all-start = ((f32[16,3,32,128]{3,2,1,0:T(8,128)}), f32[16,3,32,128]{3,2,1,0:T(8,128)S(1)}, u32[]{:S(2)}, u32[]{:S(2)}) async-start(f32[16,3,32,128]{3,2,1,0:T(8,128)} %data_sums.1), calls=%async_computation | async-start | bytes 1572864 | tf_op jit(solution)/shard_map/all_to_all | solution.py:391
  21.3 2.7 %copy-start = (f32[3,128,128]{2,1,0:T(8,128)S(1)}, f32[3,128,128]{2,1,0:T(8,128)}, u32[]{:S(2)}) copy-start(f32[3,128,128]{2,1,0:T(8,128)} %blur_ref.1) | copy-start | bytes 589828
  21.3 2.7 %copy-start.1 = (f32[3,7]{1,0:T(4,128)S(1)}, f32[3,7]{1,0:T(4,128)}, u32[]{:S(2)}) copy-start(f32[3,7]{1,0:T(4,128)} %taps_ref.3) | copy-start | bytes 256
where the time goes:
time: 41.7 us; the launch traced here: 41.3 us
  Pallas kernels  16.9 us (41%)
  starting transfers between devices  11.3 us (27%)
  waiting for transfers between devices  10.2 us (24%)
  matrix products  1.36 us (3%)
  local copies, waits for them, and re-layouts  1.22 us (3%)
    all_to_all x1, waiting for transfers between devices, shards(): received = lax.all_to_all(sums, 'gz', 0, 0, tiled=True)  10.2 us
    pallas_call x1, Pallas kernels, data_sums(): pl.pallas_call(data_kernel, out_shape=jax.ShapeDtypeStruct((chunks, bands...  9.85 us
    all_to_all x1, starting transfers between devices, shards(): received = lax.all_to_all(sums, 'gz', 0, 0, tiled=True)  5.82 us
    pallas_call x1, Pallas kernels, estimate_part(): pl.pallas_call(estimate_kernel, out_shape=jax.ShapeDtypeStruct((width, pl...  5.72 us
    ppermute x1, starting transfers between devices, halo(): lax.ppermute(estimate[:, :take], 'gz', [(s, (s - hop) % ring) for s in ra...  5.52 us
    pallas_call x1, Pallas kernels, combine(): pl.pallas_call(combine_kernel, out_shape=jax.ShapeDtypeStruct((planes * w...  1.37 us
    dynamic_slice x1, local copies, waits for them, and re-layouts, shards(): near = lax.dynamic_slice_in_dim(table, begin, width + 2 * span, axis=1)  0.99 us
    dot_general x1, matrix products, exact_dot(): jnp.dot(left_side, right_side, preferred_element_type=jnp.float32, precis...  0.99 us
  transfers between devices with their start and end apart: 3, of which 1 were waited for; matrix products, arithmetic and copies ran while one was open for 6% of the time, Pallas kernels for 14%

commit v1 on v0

--- a/solution.py
+++ b/solution.py
@@ -66,14 +66,52 @@
     return cos_one * cos_one - sin_one * sin_one, 2.0 * (sin_one * cos_one)
 
 
+def blurred(mixed, image, taps, begin, step):
+    reach = (len(taps) - 1) // 2
+    acc = None
+    for offset in range(-reach, reach + 1):
+        term = taps[offset + reach] * mixed[image, pl.ds(begin + PAD - offset, step), :]
+        acc = term if acc is None else acc + term
+    return acc
+
+
+def band_rows(mixed, images, taps, table, weight, band, begin, step):
+    at = pl.ds(begin + PAD, step)
+    parts = [wide(blurred(mixed, image, taps, begin, step)) for image in images]
+    product = narrow(wide_dot(jnp.concatenate(parts, axis=0), weight))
+    acc = None
+    for orient in range(len(images) // 2):
+        cos_pattern, sin_pattern = harmonic_of(
+            table[2 * orient, at, :], table[2 * orient + 1, at, :], band
+        )
+        even = product[2 * orient * step : (2 * orient + 1) * step]
+        odd = product[(2 * orient + 1) * step : (2 * orient + 2) * step]
+        term = cos_pattern * even - sin_pattern * odd
+        acc = term if acc is None else acc + term
+    return acc
+
+
+def put(out, index, band, values):
+    width = out.shape[2]
+    shares = values.shape[0] // width
+    for share in range(shares):
+        out[index * shares + share, band] = values[share * width : (share + 1) * width]
+
+
+def scaled_taps(taps_ref, band, count):
+    return [taps_ref[band, at] * (1.0 / count) for at in range(taps_ref.shape[1])]
+
+
 def data_kernel(
-    phase_ref, taps_ref, frames_hbm, blur_hbm, table_hbm, out_ref,
-    raw, mixed, weight, table, blur_rows, sems, side_sems,
+    phase_hbm, taps_hbm, frames_hbm, blur_hbm, table_hbm, out_hbm,
+    raw, mixed, weight, table, blur_rows, out, phase_ref, taps_ref,
+    frame_sems, side_sems, out_sems,
 ):
-    orients, phases = frames_hbm.shape[0], frames_hbm.shape[1]
+    orients, phases = raw.shape[0], raw.shape[1]
     loop_width = raw.shape[2]
-    _, bands, width, _ = out_ref.shape
-    reach = (taps_ref.shape[1] - 1) // 2
+    bands, width = out.shape[1], out.shape[2]
+    phase_copy = pltpu.make_async_copy(phase_hbm, phase_ref, side_sems.at[0])
+    phase_copy.start()
     copies = []
     for orient in range(orients):
         row = []
@@ -81,19 +119,23 @@
             copy = pltpu.make_async_copy(
                 frames_hbm.at[orient, index, 0],
                 raw.at[orient, index],
-                sems.at[orient, index],
+                frame_sems.at[orient, index],
             )
             copy.start()
             row.append(copy)
         copies.append(row)
-    blur_copy = pltpu.make_async_copy(blur_hbm, blur_rows, side_sems.at[0])
+    taps_copy = pltpu.make_async_copy(taps_hbm, taps_ref, side_sems.at[1])
+    taps_copy.start()
+    blur_copy = pltpu.make_async_copy(blur_hbm, blur_rows, side_sems.at[2])
     blur_copy.start()
-    table_copy = pltpu.make_async_copy(table_hbm, table, side_sems.at[1])
+    table_copy = pltpu.make_async_copy(table_hbm, table, side_sems.at[3])
     table_copy.start()
-    total = bands * 0 + 4 * orients
     c1, c2 = math.cos(2 * math.pi / 5), math.cos(4 * math.pi / 5)
     s1, s2 = math.sin(2 * math.pi / 5), math.sin(4 * math.pi / 5)
     step = max(64, width)
+    reach = (taps_ref.shape[1] - 1) // 2
+    total = 4 * orients
+    phase_copy.wait()
     for orient in range(orients):
         holder = []
         for step_index in range(phases):
@@ -113,10 +155,10 @@
             far = (f2 + f3).astype(jnp.float32) * data_scale - 4.0
             near_odd = (f1 - f4).astype(jnp.float32) * data_scale
             far_odd = (f2 - f3).astype(jnp.float32) * data_scale
-            mixed[4 * orient, at, :] = zero + c1 * near + c2 * far
-            mixed[4 * orient + 1, at, :] = s1 * near_odd + s2 * far_odd
-            mixed[4 * orient + 2, at, :] = zero + c2 * near + c1 * far
-            mixed[4 * orient + 3, at, :] = s2 * near_odd - s1 * far_odd
+            mixed[2 * orient, at, :] = zero + c1 * near + c2 * far
+            mixed[2 * orient + 1, at, :] = s1 * near_odd + s2 * far_odd
+            mixed[2 * (orients + orient), at, :] = zero + c2 * near + c1 * far
+            mixed[2 * (orients + orient) + 1, at, :] = s2 * near_odd - s1 * far_odd
             plain = zero + near + far
             if orient:
                 plain = plain + mixed[total, at, :]
@@ -131,77 +173,66 @@
         mixed[image, loop_width + PAD : loop_width + PAD + reach, :] = mixed[
             image, PAD : PAD + reach, :
         ]
+    taps_copy.wait()
     blur_copy.wait()
     for band in range(bands):
         weight[band] = weights(blur_rows[band])
-    table_copy.wait()
-
-    def blur(image, band, begin):
-        acc = None
-        for offset in range(-reach, reach + 1):
-            tap = taps_ref[band, offset + reach] * (1.0 / (orients * phases))
-            term = tap * mixed[image, pl.ds(begin + PAD - offset, step), :]
-            acc = term if acc is None else acc + term
-        return acc
-
-    shares = step // width
-
-    def store(index, band, values):
-        for share in range(shares):
-            out_ref[index * shares + share, band] = values[share * width : (share + 1) * width]
+    taps = [scaled_taps(taps_ref, band, orients * phases) for band in range(bands)]
 
     def plain_out(index, carry):
         begin = pl.multiple_of(index * step, step)
-        store(index, 0, narrow(wide_dot(wide(blur(total, 0, begin)), weight[0])))
+        rows = blurred(mixed, total, taps[0], begin, step)
+        put(out, index, 0, narrow(wide_dot(wide(rows), weight[0])))
         return carry
 
     lax.fori_loop(0, loop_width // step, plain_out, 0)
+    out_copies = [pltpu.make_async_copy(out.at[:, 0], out_hbm.at[:, 0], out_sems.at[0])]
+    out_copies[0].start()
+    table_copy.wait()
     for band in range(1, bands):
+        images = list(range(2 * orients * (band - 1), 2 * orients * band))
 
         def band_out(index, carry):
             begin = pl.multiple_of(index * step, step)
-            at = pl.ds(begin + PAD, step)
-            parts = []
-            for orient in range(orients):
-                for part in range(2):
-                    parts.append(wide(blur(4 * orient + 2 * band - 2 + part, band, begin)))
-            product = narrow(wide_dot(jnp.concatenate(parts, axis=0), weight[band]))
-            acc = None
-            for orient in range(orients):
-                cos_pattern, sin_pattern = harmonic_of(
-                    table[2 * orient, at, :], table[2 * orient + 1, at, :], band
-                )
-                even = product[2 * orient * step : (2 * orient + 1) * step]
-                odd = product[(2 * orient + 1) * step : (2 * orient + 2) * step]
-                term = cos_pattern * even - sin_pattern * odd
-                acc = term if acc is None else acc + term
-            store(index, band, acc)
+            put(
+                out,
+                index,
+                band,
+                band_rows(mixed, images, taps[band], table, weight[band], band, begin, step),
+            )
             return carry
 
         lax.fori_loop(0, loop_width // step, band_out, 0)
+        out_copies.append(
+            pltpu.make_async_copy(out.at[:, band], out_hbm.at[:, band], out_sems.at[band])
+        )
+        out_copies[band].start()
+    for copy in out_copies:
+        copy.wait()
 
 
 def data_sums(frames, phase_index, row_blur, column_taps, table, chunks):
     orients, phases, _, loop_width, row_count = frames.shape
     bands = row_blur.shape[0]
     width = loop_width // chunks
-    smem = pl.BlockSpec(memory_space=pltpu.SMEM)
-    vmem = pl.BlockSpec(memory_space=pltpu.VMEM)
     anywhere = pl.BlockSpec(memory_space=pltpu.HBM)
-    images = 4 * orients + 1
     return pl.pallas_call(
         data_kernel,
         out_shape=jax.ShapeDtypeStruct((chunks, bands, width, row_count), jnp.float32),
-        in_specs=[smem, smem, anywhere, anywhere, anywhere],
-        out_specs=vmem,
+        in_specs=[anywhere] * 5,
+        out_specs=anywhere,
         scratch_shapes=[
             pltpu.VMEM((orients, phases, loop_width, row_count), jnp.int32),
-            pltpu.VMEM((images, loop_width + 2 * PAD, row_count), jnp.float32),
+            pltpu.VMEM((4 * orients + 1, loop_width + 2 * PAD, row_count), jnp.float32),
             pltpu.VMEM((bands, 2 * row_count, 2 * row_count), jnp.bfloat16),
             pltpu.VMEM(table.shape, jnp.float32),
             pltpu.VMEM(row_blur.shape, jnp.float32),
+            pltpu.VMEM((chunks, bands, width, row_count), jnp.float32),
+            pltpu.SMEM(phase_index.shape, jnp.int32),
+            pltpu.SMEM(column_taps.shape, jnp.float32),
             pltpu.SemaphoreType.DMA((orients, phases)),
-            pltpu.SemaphoreType.DMA((2,)),
+            pltpu.SemaphoreType.DMA((4,)),
+            pltpu.SemaphoreType.DMA((bands,)),
         ],
         cost_estimate=pl.CostEstimate(
             flops=13 * loop_width * 2 * 256 * 256, bytes_accessed=frames.size * 4, transcendentals=0
@@ -310,9 +341,9 @@
 
 def combine_kernel(adjoint_ref, estimate_ref, received_ref, out_ref):
     width, planes, _ = estimate_ref.shape
+    depth = adjoint_ref.shape[1]
     high, low = split(adjoint_ref[...])
     left_side = jnp.concatenate([high, high, low], axis=1)
-    depth = adjoint_ref.shape[1]
     for index in range(width):
         high, low = split(received_ref[pl.ds(index, depth, stride=width), :])
         right_side = jnp.concatenate([high, low, high], axis=0)
@@ -321,14 +352,15 @@
         )
 
 
-def combine(adjoint, from_estimate, received):
+def combine(forward, from_estimate, received):
     width, planes, row_count = from_estimate.shape
-    depth = adjoint.shape[1]
+    depth = forward.shape[0] * planes
+    adjoint = forward.transpose(2, 1, 0).reshape(planes, depth)
     vmem = pl.BlockSpec(memory_space=pltpu.VMEM)
     return pl.pallas_call(
         combine_kernel,
         out_shape=jax.ShapeDtypeStruct((planes * width, row_count), jnp.float32),
-        in_specs=[vmem, vmem, vmem],
+        in_specs=[vmem] * 3,
         out_specs=vmem,
         cost_estimate=pl.CostEstimate(
             flops=2 * received.size * planes, bytes_accessed=received.size * 4, transcendentals=0
@@ -396,8 +428,7 @@
     begin = lax.axis_index("gz") * width + (PAD - span)
     near = lax.dynamic_slice_in_dim(table, begin, width + 2 * span, axis=1)
     from_estimate = estimate_part(axial, near, row_blur, column_taps, width)
-    adjoint = forward.transpose(2, 1, 0).reshape(planes, planes * bands)
-    return combine(adjoint, from_estimate, received)
+    return combine(forward, from_estimate, received)
 
 
 def solution(mesh):

time: 41.7 us -> 40.5 us (0.971)
  Pallas kernels: 16.9 us -> 15.8 us
    pallas_call x1, Pallas kernels: 9.85 us -> 8.72 us  [data_sums(): pl.pallas_call(data_kernel, out_shape=jax.ShapeDtypeStruct((chunks, bands...]
where the time goes in v1:
time: 40.5 us; the launch traced here: 40.2 us
  Pallas kernels  15.8 us (39%)
  starting transfers between devices  11.3 us (28%)
  waiting for transfers between devices  10.2 us (25%)
  matrix products  1.36 us (3%)
  local copies, waits for them, and re-layouts  1.22 us (3%)
    all_to_all x1, waiting for transfers between devices, shards(): received = lax.all_to_all(sums, 'gz', 0, 0, tiled=True)  10.2 us
    pallas_call x1, Pallas kernels, data_sums(): pl.pallas_call(data_kernel, out_shape=jax.ShapeDtypeStruct((chunks, bands...  8.72 us
    all_to_all x1, starting transfers between devices, shards(): received = lax.all_to_all(sums, 'gz', 0, 0, tiled=True)  5.82 us
    pallas_call x1, Pallas kernels, estimate_part(): pl.pallas_call(estimate_kernel, out_shape=jax.ShapeDtypeStruct((width, pl...  5.72 us
    ppermute x1, starting transfers between devices, halo(): lax.ppermute(estimate[:, :take], 'gz', [(s, (s - hop) % ring) for s in ra...  5.52 us
    pallas_call x1, Pallas kernels, combine(): pl.pallas_call(combine_kernel, out_shape=jax.ShapeDtypeStruct((planes * w...  1.37 us
    dynamic_slice x1, local copies, waits for them, and re-layouts, shards(): near = lax.dynamic_slice_in_dim(table, begin, width + 2 * span, axis=1)  0.99 us
    dot_general x1, matrix products, exact_dot(): jnp.dot(left_side, right_side, preferred_element_type=jnp.float32, precis...  0.99 us
  transfers between devices with their start and end apart: 3, of which 1 were waited for; matrix products, arithmetic and copies ran while one was open for 6% of the time, Pallas kernels for 14%

profile of v1, /device:TPU:0, one launch (start us, length us, event | category | flops | bytes accessed | tf_op | source)
XLA Modules:
  0.0 40.2 jit_solution(17336311686016639934)
XLA Ops:
  0.0 0.0 copy-start.2
  0.0 8.7 %data_sums.1 = f32[16,3,32,128]{3,2,1,0:T(8,128)} custom-call(s32[3,5]{1,0:T(4,128)} %phase_hbm.1, f32[3,7]{1,0:T(4,128)} %taps_ref.1, s32[3,5,1,512,128]{4,3,2,1,0:T(8,128)} %frames_hbm.1, f32[3,128,128]{2,1,0:T(8,128)} %blur_ref.1, f32[6,528,128]{2,1,0:T(8,128)} %constant.21.clone.table_hbm), custom_call_target="tpu_custom_call" | custom-call | flops 872415232 | bytes 3932160 | tf_op jit(solution)/shard_map/data_sums/pallas_call | solution.py:219
  8.7 0.0 copy-done.2
  8.7 0.0 copy-start.6
  8.8 0.0 copy-start.4
  8.8 0.0 copy-start.5
  8.8 0.0 copy-start.3
  8.8 5.5 %collective-permute-start.1 = (f32[16,6,128]{2,1,0:T(8,128)S(1)}, f32[16,6,128]{2,1,0:T(8,128)S(1)}, u32[]{:S(2)}, u32[]{:S(2)}) collective-permute-start(f32[16,6,128]{2,1,0:T(8,128)S(1)} %get-tuple-element.10), channel_id=1, source_target_pairs={{0,15},{1,0},{2,1},{3,2},{4,3},{5,4},{6,5},{7,6},{8,7},{9,8},{10,9... | collective-permute-start | bytes 147464 | tf_op jit(solution)/shard_map/ppermute | solution.py:389
  14.3 0.0 collective-permute-start
  14.3 5.8 %all-to-all-start = ((f32[16,3,32,128]{3,2,1,0:T(8,128)}), f32[16,3,32,128]{3,2,1,0:T(8,128)S(1)}, u32[]{:S(2)}, u32[]{:S(2)}) async-start(f32[16,3,32,128]{3,2,1,0:T(8,128)} %data_sums.1), calls=%async_computation | async-start | bytes 1572864 | tf_op jit(solution)/shard_map/all_to_all | solution.py:423
  20.2 0.0 copy-start
  20.2 0.0 copy-start.1
  20.2 0.0 copy-done.6
  20.2 1.0 %constant_dynamic-slice_fusion.table_ref = f32[6,44,128]{2,1,0:T(8,128)S(1)} fusion(f32[6,528,128]{2,1,0:T(8,128)} %constant.21.clone.table_hbm, s32[]{:T(128)S(6)} %select_n.3), kind=kLoop, calls=%fused_computation.14 | loop fusion | bytes 270340 | tf_op jit(solution)/shard_map/dynamic_slice | solution.py:429
  21.2 0.0 copy-done.4
  21.2 0.0 copy-done.5
  21.3 0.0 copy-done.3
  21.3 0.2 fusion.1
  21.5 0.2 convolution_bitcast_fusion.1
  21.7 0.1 copy.12
  21.8 0.1 copy.14.adjoint_ref
  21.8 0.0 collective-permute-done.1
  21.8 0.0 collective-permute-done
  21.8 0.1 pad_maximum_fusion
  21.9 1.0 %convolution_bitcast_fusion.axial_ref = f32[3,44,16,128]{3,2,1,0:T(8,128)S(1)} fusion(f32[3,16,16,1]{2,1,3,0:T(8,128)S(1)} %convolution_bitcast_fusion.1, f32[2,8,44,128]{3,2,1,0:T(8,128)S(1)} %bitcast.37), kind=kOutput, calls=%fused_computation | convolution fusion | flops 51904512 | bytes 1444864 | tf_op jit(solution)/shard_map/dot_general | solution.py:19
  22.9 0.0 copy-done
  22.9 0.0 copy-done.1
  22.9 5.7 %estimate_part.1.estimate_ref = f32[32,16,128]{2,1,0:T(8,128)S(1)} custom-call(f32[3,7]{1,0:T(4,128)S(1)} %copy-done.1, f32[3,44,16,128]{3,2,1,0:T(8,128)S(1)} %convolution_bitcast_fusion.axial_ref, f32[6,44,128]{2,1,0:T(8,128)S(1)} %constant_dynamic-slice_fusion.table_ref, f32[3,128,128]{2,1,0:T(8,128)S(1)} %copy-done), custom_call_target="tpu_custom_call" | custom-call | flops 16106127360 | bytes 1081344 | tf_op jit(solution)/shard_map/estimate_part/pallas_call | solution.py:329
  28.6 10.2 %all-to-all-done = f32[16,3,32,128]{3,2,1,0:T(8,128)S(1)} async-done(((f32[16,3,32,128]{3,2,1,0:T(8,128)}), f32[16,3,32,128]{3,2,1,0:T(8,128)S(1)}, u32[]{:S(2)}, u32[]{:S(2)}) %all-to-all-start) | async-done | bytes 786464 | tf_op jit(solution)/shard_map/all_to_all | solution.py:423
  38.8 1.4 %combine.1 = f32[512,128]{1,0:T(8,128)} custom-call(f32[16,48]{1,0:T(8,128)S(1)} %copy.14.adjoint_ref, f32[32,16,128]{2,1,0:T(8,128)S(1)} %estimate_part.1.estimate_ref, f32[1536,128]{1,0:T(8,128)S(1)} %bitcast.36), custom_call_target="tpu_custom_call" | custom-call | flops 6291456 | bytes 786432 | tf_op jit(solution)/shard_map/combine/pallas_call | solution.py:360
  (5 shorter events, 0.1 us)
Async XLA Ops:
  0.0 8.7 %copy-start.2 = (f32[16,32,128]{2,1,0:T(8,128)S(1)}, f32[16,32,128]{2,1,0:T(8,128)}, u32[]{:S(2)}) copy-start(f32[16,32,128]{2,1,0:T(8,128)} %param.10) | copy-start | bytes 786436
  8.7 11.5 %copy-start.6 = (f32[3,2,16]{2,1,0:T(2,128)S(1)}, f32[3,2,16]{2,1,0:T(2,128)}, u32[]{:S(2)}) copy-start(f32[3,2,16]{2,1,0:T(2,128)} %param.13) | copy-start | bytes 1156
  8.8 12.5 %copy-start.4 = (f32[16,16]{0,1:T(8,128)S(1)}, f32[16,16]{0,1:T(8,128)}, u32[]{:S(2)}) copy-start(f32[16,16]{0,1:T(8,128)} %constant.23.clone) | copy-start | bytes 3076
  8.8 12.5 %copy-start.5 = (f32[16,16]{0,1:T(8,128)S(1)}, f32[16,16]{0,1:T(8,128)}, u32[]{:S(2)}) copy-start(f32[16,16]{0,1:T(8,128)} %constant.22.clone) | copy-start | bytes 3076
  8.8 12.5 %copy-start.3 = (f32[16,32,1]{1,0,2:T(8,128)S(1)}, f32[16,32,1]{1,0,2:T(8,128)}, u32[]{:S(2)}) copy-start(f32[16,32,1]{1,0,2:T(8,128)} %constant.26) | copy-start | bytes 6148
  8.8 13.0 %collective-permute-start.1 = (f32[16,6,128]{2,1,0:T(8,128)S(1)}, f32[16,6,128]{2,1,0:T(8,128)S(1)}, u32[]{:S(2)}, u32[]{:S(2)}) collective-permute-start(f32[16,6,128]{2,1,0:T(8,128)S(1)} %get-tuple-element.10), channel_id=1, source_target_pairs={{0,15},{1,0},{2,1},{3,2},{4,3},{5,4},{6,5},{7,6},{8,7},{9,8},{10,9... | collective-permute-start | bytes 147464 | tf_op jit(solution)/shard_map/ppermute | solution.py:389
  14.3 7.5 %collective-permute-start = (f32[16,6,128]{2,1,0:T(8,128)S(1)}, f32[16,6,128]{2,1,0:T(8,128)S(1)}, u32[]{:S(2)}, u32[]{:S(2)}) collective-permute-start(f32[16,6,128]{2,1,0:T(8,128)S(1)} %get-tuple-element.9), channel_id=1, source_target_pairs={{0,1},{1,2},{2,3},{3,4},{4,5},{5,6},{6,7},{7,8},{8,9},{9,10},{10,1... | collective-permute-start | bytes 147464 | tf_op jit(solution)/shard_map/ppermute | solution.py:384
  14.3 24.5 %all-to-all-start = ((f32[16,3,32,128]{3,2,1,0:T(8,128)}), f32[16,3,32,128]{3,2,1,0:T(8,128)S(1)}, u32[]{:S(2)}, u32[]{:S(2)}) async-start(f32[16,3,32,128]{3,2,1,0:T(8,128)} %data_sums.1), calls=%async_computation | async-start | bytes 1572864 | tf_op jit(solution)/shard_map/all_to_all | solution.py:423
  20.2 2.7 %copy-start = (f32[3,128,128]{2,1,0:T(8,128)S(1)}, f32[3,128,128]{2,1,0:T(8,128)}, u32[]{:S(2)}) copy-start(f32[3,128,128]{2,1,0:T(8,128)} %blur_ref.1) | copy-start | bytes 589828
  20.2 2.7 %copy-start.1 = (f32[3,7]{1,0:T(4,128)S(1)}, f32[3,7]{1,0:T(4,128)}, u32[]{:S(2)}) copy-start(f32[3,7]{1,0:T(4,128)} %taps_ref.1) | copy-start | bytes 256

commit v2 on v1

--- a/solution.py
+++ b/solution.py
@@ -1,3 +1,4 @@
+import functools
 import math
 
 import jax
@@ -46,8 +47,8 @@
     return jnp.dot(left_side, right_side, preferred_element_type=jnp.float32)
 
 
-def pattern_table(orients, loop_width, row_count):
-    columns = np.arange(-PAD, loop_width + PAD) % loop_width
+def pattern_table(orients, loop_width, row_count, pad):
+    columns = np.arange(-pad, loop_width + pad) % loop_width
     rows = np.arange(row_count)
     images = []
     for orient in range(orients):
@@ -76,8 +77,8 @@
 
 
 def band_rows(mixed, images, taps, table, weight, band, begin, step):
-    at = pl.ds(begin + PAD, step)
-    parts = [wide(blurred(mixed, image, taps, begin, step)) for image in images]
+    at = pl.ds(begin + (table.shape[1] - mixed.shape[1]) // 2 + PAD, step)
+    parts = [wide(blurred(mixed, image, cut, begin, step)) for image, cut in zip(images, taps)]
     product = narrow(wide_dot(jnp.concatenate(parts, axis=0), weight))
     acc = None
     for orient in range(len(images) // 2):
@@ -98,18 +99,18 @@
         out[index * shares + share, band] = values[share * width : (share + 1) * width]
 
 
-def scaled_taps(taps_ref, band, count):
-    return [taps_ref[band, at] * (1.0 / count) for at in range(taps_ref.shape[1])]
+def scaled_taps(taps_ref, band, scale):
+    return [taps_ref[band, at] * scale for at in range(taps_ref.shape[1])]
 
 
 def data_kernel(
     phase_hbm, taps_hbm, frames_hbm, blur_hbm, table_hbm, out_hbm,
-    raw, mixed, weight, table, blur_rows, out, phase_ref, taps_ref,
+    raw, summed, mixed, weight, table, blur_rows, out, phase_ref, taps_ref,
     frame_sems, side_sems, out_sems,
 ):
     orients, phases = raw.shape[0], raw.shape[1]
     loop_width = raw.shape[2]
-    bands, width = out.shape[1], out.shape[2]
+    bands = out.shape[1]
     phase_copy = pltpu.make_async_copy(phase_hbm, phase_ref, side_sems.at[0])
     phase_copy.start()
     copies = []
@@ -130,11 +131,12 @@
     blur_copy.start()
     table_copy = pltpu.make_async_copy(table_hbm, table, side_sems.at[3])
     table_copy.start()
-    c1, c2 = math.cos(2 * math.pi / 5), math.cos(4 * math.pi / 5)
-    s1, s2 = math.sin(2 * math.pi / 5), math.sin(4 * math.pi / 5)
-    step = max(64, width)
+    step = loop_width // 2
     reach = (taps_ref.shape[1] - 1) // 2
     total = 4 * orients
+    count = orients * phases
+    first_sine, second_sine = math.sin(2 * math.pi / 5), math.sin(4 * math.pi / 5)
+    ratio = second_sine / first_sine
     phase_copy.wait()
     for orient in range(orients):
         holder = []
@@ -150,19 +152,23 @@
             rows = pl.ds(pl.multiple_of(index * step, step), step)
             at = pl.ds(pl.multiple_of(index * step + PAD, 8), step)
             f0, f1, f2, f3, f4 = [raw[orient, k, rows, :] for k in holder]
-            zero = f0.astype(jnp.float32) * data_scale - 2.0
-            near = (f1 + f4).astype(jnp.float32) * data_scale - 4.0
-            far = (f2 + f3).astype(jnp.float32) * data_scale - 4.0
-            near_odd = (f1 - f4).astype(jnp.float32) * data_scale
-            far_odd = (f2 - f3).astype(jnp.float32) * data_scale
-            mixed[2 * orient, at, :] = zero + c1 * near + c2 * far
-            mixed[2 * orient + 1, at, :] = s1 * near_odd + s2 * far_odd
-            mixed[2 * (orients + orient), at, :] = zero + c2 * near + c1 * far
-            mixed[2 * (orients + orient) + 1, at, :] = s2 * near_odd - s1 * far_odd
-            plain = zero + near + far
+            near, far, near_odd, far_odd = f1 + f4, f2 + f3, f1 - f4, f2 - f3
+            both = near + far
+            even = (4 * f0 - both).astype(jnp.float32)
+            swing = (near - far).astype(jnp.float32) * math.sqrt(5.0)
+            near_odd = near_odd.astype(jnp.float32)
+            far_odd = far_odd.astype(jnp.float32)
+            mixed[2 * orient, at, :] = even + swing
+            mixed[2 * orient + 1, at, :] = near_odd + ratio * far_odd
+            mixed[2 * (orients + orient), at, :] = even - swing
+            mixed[2 * (orients + orient) + 1, at, :] = ratio * near_odd - far_odd
+            plain = f0 + both
             if orient:
-                plain = plain + mixed[total, at, :]
-            mixed[total, at, :] = plain
+                plain = plain + summed[rows, :]
+            if orient < orients - 1:
+                summed[rows, :] = plain
+            else:
+                mixed[total, at, :] = plain.astype(jnp.float32) * data_scale - 2.0 * count
             return carry
 
         lax.fori_loop(0, loop_width // step, mix, 0)
@@ -177,7 +183,13 @@
     blur_copy.wait()
     for band in range(bands):
         weight[band] = weights(blur_rows[band])
-    taps = [scaled_taps(taps_ref, band, orients * phases) for band in range(bands)]
+    even_scale, odd_scale = data_scale / (4.0 * count), data_scale * first_sine / count
+    taps = [scaled_taps(taps_ref, 0, 1.0 / count)]
+    for band in range(1, bands):
+        taps.append(
+            [scaled_taps(taps_ref, band, even_scale), scaled_taps(taps_ref, band, odd_scale)]
+            * orients
+        )
 
     def plain_out(index, carry):
         begin = pl.multiple_of(index * step, step)
@@ -223,6 +235,7 @@
         out_specs=anywhere,
         scratch_shapes=[
             pltpu.VMEM((orients, phases, loop_width, row_count), jnp.int32),
+            pltpu.VMEM((loop_width, row_count), jnp.int32),
             pltpu.VMEM((4 * orients + 1, loop_width + 2 * PAD, row_count), jnp.float32),
             pltpu.VMEM((bands, 2 * row_count, 2 * row_count), jnp.bfloat16),
             pltpu.VMEM(table.shape, jnp.float32),
@@ -244,7 +257,6 @@
 
 def estimate_kernel(taps_ref, axial_ref, table_ref, blur_ref, out_ref):
     bands, _, planes, _ = axial_ref.shape
-    width = out_ref.shape[0]
     orients = table_ref.shape[0] // 2
     reach = (taps_ref.shape[1] - 1) // 2
     span = 2 * reach
@@ -317,12 +329,13 @@
             out_ref[begin + i] = acc[i]
         return carry
 
-    lax.fori_loop(0, width // step, chunk, 0)
-
-
-def estimate_part(axial, table, row_blur, column_taps, width):
-    _, _, planes, row_count = axial.shape
+    lax.fori_loop(0, out_ref.shape[0] // step, chunk, 0)
+
+
+def estimate_part(axial, table, row_blur, column_taps):
+    _, padded, planes, row_count = axial.shape
     orients = table.shape[0] // 2
+    width = padded - 2 * (column_taps.shape[1] - 1)
     smem = pl.BlockSpec(memory_space=pltpu.SMEM)
     vmem = pl.BlockSpec(memory_space=pltpu.VMEM)
     rows = 2 * orients * width * planes
@@ -339,58 +352,62 @@
     )(column_taps, axial, table, row_blur)
 
 
-def combine_kernel(adjoint_ref, estimate_ref, received_ref, out_ref):
-    width, planes, _ = estimate_ref.shape
+def combine_kernel(adjoint_ref, estimate_ref, received_ref, *refs, places):
+    out_ref = refs[-1]
+    planes, _ = estimate_ref.shape[1:]
     depth = adjoint_ref.shape[1]
+    width = received_ref.shape[0] // depth
+    span = (estimate_ref.shape[0] - width) // 2
     high, low = split(adjoint_ref[...])
     left_side = jnp.concatenate([high, high, low], axis=1)
     for index in range(width):
         high, low = split(received_ref[pl.ds(index, depth, stride=width), :])
         right_side = jnp.concatenate([high, low, high], axis=0)
-        out_ref[pl.ds(index, planes, stride=width), :] = estimate_ref[index] - wide_dot(
-            left_side, right_side
-        )
-
-
-def combine(forward, from_estimate, received):
-    width, planes, row_count = from_estimate.shape
+        acc = estimate_ref[span + index]
+        for ref, (begin, count) in zip(refs, places):
+            if begin <= index < begin + count:
+                acc = acc + ref[index - begin]
+        out_ref[pl.ds(index, planes, stride=width), :] = acc - wide_dot(left_side, right_side)
+
+
+def combine(forward, from_estimate, pieces, places, received):
+    planes, row_count = from_estimate.shape[1:]
     depth = forward.shape[0] * planes
+    width = received.size // (depth * row_count)
     adjoint = forward.transpose(2, 1, 0).reshape(planes, depth)
     vmem = pl.BlockSpec(memory_space=pltpu.VMEM)
     return pl.pallas_call(
-        combine_kernel,
+        functools.partial(combine_kernel, places=places),
         out_shape=jax.ShapeDtypeStruct((planes * width, row_count), jnp.float32),
-        in_specs=[vmem] * 3,
+        in_specs=[vmem] * (3 + len(pieces)),
         out_specs=vmem,
         cost_estimate=pl.CostEstimate(
             flops=2 * received.size * planes, bytes_accessed=received.size * 4, transcendentals=0
         ),
         compiler_params=pltpu.CompilerParams(vmem_limit_bytes=24 << 20),
         name="combine",
-    )(adjoint, from_estimate, received.reshape(depth * width, row_count)).reshape(
+    )(adjoint, from_estimate, received.reshape(depth * width, row_count), *pieces).reshape(
         planes, width, row_count
     )
 
 
-def halo(estimate, span):
+def spread(from_estimate, span):
     ring = lax.axis_size("gz")
-    width = estimate.shape[1]
-    lefts, rights = [], []
+    width = from_estimate.shape[0] - 2 * span
+    pieces, places = [], []
     hop, missing = 1, span
     while missing > 0:
         take = min(missing, width)
-        lefts.insert(
-            0,
-            lax.ppermute(
-                estimate[:, width - take :], "gz", [(s, (s + hop) % ring) for s in range(ring)]
-            ),
-        )
-        rights.append(
-            lax.ppermute(estimate[:, :take], "gz", [(s, (s - hop) % ring) for s in range(ring)])
-        )
+        piece = from_estimate[missing - take : missing]
+        pieces.append(lax.ppermute(piece, "gz", [(s, (s - hop) % ring) for s in range(ring)]))
+        places.append((width - take, take))
+        begin = span + width * hop
+        piece = from_estimate[begin : begin + take]
+        pieces.append(lax.ppermute(piece, "gz", [(s, (s + hop) % ring) for s in range(ring)]))
+        places.append((0, take))
         missing -= take
         hop += 1
-    return jnp.concatenate(lefts + [estimate] + rights, axis=1)
+    return pieces, places
 
 
 def axial_matrices(axial_otf, planes):
@@ -416,19 +433,20 @@
     orients = frames.shape[0]
     bands = row_blur.shape[0]
     span = column_taps.shape[1] - 1
-    table = jnp.asarray(pattern_table(orients, width * ring, row_count))
+    pad = -(-2 * span // 8) * 8
+    table = jnp.asarray(pattern_table(orients, width * ring, row_count, pad))
     sums = data_sums(frames, phase_index, row_blur, column_taps, table, ring)
-    estimate, sums = lax.optimization_barrier((estimate, sums))
-    extended = halo(estimate, span)
     received = lax.all_to_all(sums, "gz", 0, 0, tiled=True)
     forward = axial_matrices(axial_otf, planes)
     squared = jnp.einsum("mzw,mzv->mwv", forward, forward, precision=lax.Precision.HIGHEST)
-    axial = exact_dot(squared.reshape(bands * planes, planes), extended.reshape(planes, -1))
-    axial = axial.reshape(bands, planes, width + 2 * span, row_count).transpose(0, 2, 1, 3)
-    begin = lax.axis_index("gz") * width + (PAD - span)
-    near = lax.dynamic_slice_in_dim(table, begin, width + 2 * span, axis=1)
-    from_estimate = estimate_part(axial, near, row_blur, column_taps, width)
-    return combine(forward, from_estimate, received)
+    axial = exact_dot(squared.reshape(bands * planes, planes), estimate.reshape(planes, -1))
+    axial = axial.reshape(bands, planes, width, row_count).transpose(0, 2, 1, 3)
+    axial = jnp.pad(axial, ((0, 0), (2 * span, 2 * span), (0, 0), (0, 0)))
+    begin = lax.axis_index("gz") * width + (pad - 2 * span)
+    near = lax.dynamic_slice_in_dim(table, begin, width + 4 * span, axis=1)
+    from_estimate = estimate_part(axial, near, row_blur, column_taps)
+    pieces, places = spread(from_estimate, span)
+    return combine(forward, from_estimate, pieces, places, received)
 
 
 def solution(mesh):

time: 40.5 us -> 36.3 us (0.90)
  waiting for transfers between devices: 10.2 us -> 6.14 us
  starting transfers between devices: 11.3 us -> 12 us
  Pallas kernels: 15.8 us -> 15.3 us
    all_to_all x1, waiting for transfers between devices: 10.2 us -> 0.01 us  [shards(): received = lax.all_to_all(sums, 'gz', 0, 0, tiled=True)]
    ppermute x2, waiting for transfers between devices: 0.01 us -> 6.14 us  [the longest x1 4.56 us: spread(): lax.ppermute(piece, 'gz', [(s, (s + hop) % ring) for s in range(ring)])]
    pallas_call x1, Pallas kernels: 8.72 us -> 6.39 us  [data_sums(): pl.pallas_call(data_kernel, out_shape=jax.ShapeDtypeStruct((chunks, bands...]
    pallas_call x1, Pallas kernels: 5.72 us -> 7.51 us  [estimate_part(): pl.pallas_call(estimate_kernel, out_shape=jax.ShapeDtypeStruct((width, pl...]
    all_to_all x1, starting transfers between devices: 5.82 us -> 7.56 us  [shards(): received = lax.all_to_all(sums, 'gz', 0, 0, tiled=True)]
    ppermute x2, starting transfers between devices: 5.53 us -> 4.39 us  [the longest x1 4.39 us: spread(): lax.ppermute(piece, 'gz', [(s, (s - hop) % ring) for s in range(ring)])]
  transfers between devices with their start and end apart: 3 -> 3, of which waited for: 1 -> 2; matrix products, arithmetic and copies ran while one was open for 6% -> 7% of each run, Pallas kernels for 14% -> 21%
where the time goes in v2:
time: 36.3 us; the launch traced here: 36.1 us
  Pallas kernels  15.3 us (42%)
  starting transfers between devices  12 us (33%)
  waiting for transfers between devices  6.14 us (17%)
  local copies, waits for them, and re-layouts  1.28 us (4%)
  matrix products  1.19 us (3%)
    all_to_all x1, starting transfers between devices, shards(): received = lax.all_to_all(sums, 'gz', 0, 0, tiled=True)  7.56 us
    pallas_call x1, Pallas kernels, estimate_part(): pl.pallas_call(estimate_kernel, out_shape=jax.ShapeDtypeStruct((width, pl...  7.51 us
    pallas_call x1, Pallas kernels, data_sums(): pl.pallas_call(data_kernel, out_shape=jax.ShapeDtypeStruct((chunks, bands...  6.39 us
    ppermute x1, waiting for transfers between devices, spread(): lax.ppermute(piece, 'gz', [(s, (s + hop) % ring) for s in range(ring)])  4.56 us
    ppermute x1, starting transfers between devices, spread(): lax.ppermute(piece, 'gz', [(s, (s - hop) % ring) for s in range(ring)])  4.39 us
    ppermute x1, waiting for transfers between devices, spread(): lax.ppermute(piece, 'gz', [(s, (s - hop) % ring) for s in range(ring)])  1.58 us
    pallas_call x1, Pallas kernels, combine(): pl.pallas_call(functools.partial(combine_kernel, places=places), out_shap...  1.37 us
    dynamic_slice x1, local copies, waits for them, and re-layouts, shards(): near = lax.dynamic_slice_in_dim(table, begin, width + 4 * span, axis=1)  0.96 us
  transfers between devices with their start and end apart: 3, of which 2 were waited for; matrix products, arithmetic and copies ran while one was open for 7% of the time, Pallas kernels for 21%

profile of v2, /device:TPU:0, one launch (start us, length us, event | category | flops | bytes accessed | tf_op | source)
XLA Modules:
  0.0 36.1 jit_solution(6778486548322603887)
XLA Ops:
  0.0 0.0 copy-start.4
  0.0 0.0 copy-start.5
  0.0 0.0 copy-start.6
  0.0 6.4 %data_sums.1 = f32[16,3,32,128]{3,2,1,0:T(8,128)} custom-call(s32[3,5]{1,0:T(4,128)} %phase_hbm.1, f32[3,7]{1,0:T(4,128)} %taps_hbm.1, s32[3,5,1,512,128]{4,3,2,1,0:T(8,128)} %frames_hbm.1, f32[3,128,128]{2,1,0:T(8,128)} %blur_hbm.1, f32[6,544,128]{2,1,0:T(8,128)} %constant.23.clone.table_hbm), custom_call_target="tpu_custom_call" | custom-call | flops 872415232 | bytes 3932160 | tf_op jit(solution)/shard_map/data_sums/pallas_call | solution.py:231
  6.4 0.0 copy-start.3
  6.4 0.0 copy-start.2
  6.4 7.6 %all-to-all-start = ((f32[16,3,32,128]{3,2,1,0:T(8,128)}), f32[16,3,32,128]{3,2,1,0:T(8,128)S(1)}, u32[]{:S(2)}, u32[]{:S(2)}) async-start(f32[16,3,32,128]{3,2,1,0:T(8,128)} %data_sums.1), calls=%async_computation | async-start | bytes 1572864 | tf_op jit(solution)/shard_map/all_to_all | solution.py:439
  14.0 0.0 copy-done.6
  14.0 0.0 copy-done.4
  14.0 0.0 copy-done.5
  14.1 0.0 copy-done.3
  14.1 0.2 fusion.1
  14.3 0.2 convolution_bitcast_fusion.1
  14.5 1.0 %constant_dynamic-slice_fusion.table_ref = f32[6,56,128]{2,1,0:T(8,128)S(1)} fusion(f32[6,544,128]{2,1,0:T(8,128)} %constant.23.clone.table_hbm, s32[]{:T(128)S(6)} %select_n.3), kind=kLoop, calls=%fused_computation.13 | loop fusion | bytes 344068 | tf_op jit(solution)/shard_map/dynamic_slice | solution.py:446
  15.4 0.0 copy-start
  15.5 0.0 copy-start.1
  15.5 0.0 copy-done.2
  15.5 0.8 %convolution_bitcast_fusion = f32[3,32,16,128]{3,2,1,0:T(8,128)S(1)} fusion(f32[3,16,16,1]{2,1,3,0:T(8,128)S(1)} %convolution_bitcast_fusion.1, f32[2,8,32,128]{3,2,1,0:T(8,128)S(1)} %bitcast.38), kind=kOutput, calls=%fused_computation | convolution fusion | flops 37748736 | bytes 1051648 | tf_op jit(solution)/shard_map/dot_general | solution.py:20
  16.3 0.1 pad.4.axial_ref
  16.4 0.0 copy-done
  16.4 0.0 copy-done.1
  16.4 7.5 %estimate_part.1.estimate_ref = f32[44,16,128]{2,1,0:T(8,128)S(1)} custom-call(f32[3,7]{1,0:T(4,128)S(1)} %copy-done.1, f32[3,56,16,128]{3,2,1,0:T(8,128)S(1)} %pad.4.axial_ref, f32[6,56,128]{2,1,0:T(8,128)S(1)} %constant_dynamic-slice_fusion.table_ref, f32[3,128,128]{2,1,0:T(8,128)S(1)} %copy-done), custom_call_target="tpu_custom_call" | custom-call | flops 22145925120 | bytes 1376256 | tf_op jit(solution)/shard_map/estimate_part/pallas_call | solution.py:342
  24.0 4.4 %collective-permute-start = (f32[6,16,128]{2,1,0:T(8,128)S(1)}, f32[6,16,128]{2,1,0:T(8,128)S(1)}, u32[]{:S(2)}, u32[]{:S(2)}) collective-permute-start(f32[6,16,128]{2,1,0:T(8,128)S(1)} %get-tuple-element.6), channel_id=1, source_target_pairs={{0,15},{1,0},{2,1},{3,2},{4,3},{5,4},{6,5},{7,6},{8,7},{9,8},{10,9... | collective-permute-start | bytes 147464 | tf_op jit(solution)/shard_map/ppermute | solution.py:402
  28.4 0.0 collective-permute-start.1
  28.4 0.1 copy.12
  28.5 0.1 copy.14.adjoint_ref
  28.5 1.6 %collective-permute-done.refs_0_ = f32[6,16,128]{2,1,0:T(8,128)S(1)} collective-permute-done((f32[6,16,128]{2,1,0:T(8,128)S(1)}, f32[6,16,128]{2,1,0:T(8,128)S(1)}, u32[]{:S(2)}, u32[]{:S(2)}) %collective-permute-start) | collective-permute-done | bytes 49184 | tf_op jit(solution)/shard_map/ppermute | solution.py:402
  30.1 4.6 %collective-permute-done.1.refs_1_ = f32[6,16,128]{2,1,0:T(8,128)S(1)} collective-permute-done((f32[6,16,128]{2,1,0:T(8,128)S(1)}, f32[6,16,128]{2,1,0:T(8,128)S(1)}, u32[]{:S(2)}, u32[]{:S(2)}) %collective-permute-start.1) | collective-permute-done | bytes 49184 | tf_op jit(solution)/shard_map/ppermute | solution.py:406
  34.7 0.0 all-to-all-done
  34.7 1.4 %combine.1 = f32[512,128]{1,0:T(8,128)} custom-call(f32[16,48]{1,0:T(8,128)S(1)} %copy.14.adjoint_ref, f32[44,16,128]{2,1,0:T(8,128)S(1)} %estimate_part.1.estimate_ref, f32[1536,128]{1,0:T(8,128)S(1)} %bitcast.36, f32[6,16,128]{2,1,0:T(8,128)S(1)} %collective-permute-done.refs_0_, f32[6,16,128]{2,1,0:T(8,128)S(1)} %collective-permute-done.1.refs_1_), custom_call_target="tpu_custom_call" | custom-call | flops 6291456 | bytes 786432 | tf_op jit(solution)/shard_map/combine/pallas_call | solution.py:379
  (5 shorter events, 0.0 us)
Async XLA Ops:
  0.0 14.0 %copy-start.4 = (f32[16,16]{0,1:T(8,128)S(1)}, f32[16,16]{0,1:T(8,128)}, u32[]{:S(2)}) copy-start(f32[16,16]{0,1:T(8,128)} %constant.25.clone) | copy-start | bytes 3076
  0.0 14.0 %copy-start.5 = (f32[16,16]{0,1:T(8,128)S(1)}, f32[16,16]{0,1:T(8,128)}, u32[]{:S(2)}) copy-start(f32[16,16]{0,1:T(8,128)} %constant.24.clone) | copy-start | bytes 3076
  0.0 14.0 %copy-start.6 = (f32[3,2,16]{2,1,0:T(2,128)S(1)}, f32[3,2,16]{2,1,0:T(2,128)}, u32[]{:S(2)}) copy-start(f32[3,2,16]{2,1,0:T(2,128)} %param.13) | copy-start | bytes 1156
  6.4 7.7 %copy-start.3 = (f32[16,32,1]{1,0,2:T(8,128)S(1)}, f32[16,32,1]{1,0,2:T(8,128)}, u32[]{:S(2)}) copy-start(f32[16,32,1]{1,0,2:T(8,128)} %constant.30) | copy-start | bytes 6148
  6.4 9.1 %copy-start.2 = (f32[16,32,128]{2,1,0:T(8,128)S(1)}, f32[16,32,128]{2,1,0:T(8,128)}, u32[]{:S(2)}) copy-start(f32[16,32,128]{2,1,0:T(8,128)} %param.10) | copy-start | bytes 786436
  6.4 28.2 %all-to-all-start = ((f32[16,3,32,128]{3,2,1,0:T(8,128)}), f32[16,3,32,128]{3,2,1,0:T(8,128)S(1)}, u32[]{:S(2)}, u32[]{:S(2)}) async-start(f32[16,3,32,128]{3,2,1,0:T(8,128)} %data_sums.1), calls=%async_computation | async-start | bytes 1572864 | tf_op jit(solution)/shard_map/all_to_all | solution.py:439
  15.4 1.0 %copy-start = (f32[3,128,128]{2,1,0:T(8,128)S(1)}, f32[3,128,128]{2,1,0:T(8,128)}, u32[]{:S(2)}) copy-start(f32[3,128,128]{2,1,0:T(8,128)} %blur_hbm.1) | copy-start | bytes 589828
  15.5 1.0 %copy-start.1 = (f32[3,7]{1,0:T(4,128)S(1)}, f32[3,7]{1,0:T(4,128)}, u32[]{:S(2)}) copy-start(f32[3,7]{1,0:T(4,128)} %taps_hbm.1) | copy-start | bytes 256
  24.0 6.1 %collective-permute-start = (f32[6,16,128]{2,1,0:T(8,128)S(1)}, f32[6,16,128]{2,1,0:T(8,128)S(1)}, u32[]{:S(2)}, u32[]{:S(2)}) collective-permute-start(f32[6,16,128]{2,1,0:T(8,128)S(1)} %get-tuple-element.6), channel_id=1, source_target_pairs={{0,15},{1,0},{2,1},{3,2},{4,3},{5,4},{6,5},{7,6},{8,7},{9,8},{10,9... | collective-permute-start | bytes 147464 | tf_op jit(solution)/shard_map/ppermute | solution.py:402
  28.4 6.3 %collective-permute-start.1 = (f32[6,16,128]{2,1,0:T(8,128)S(1)}, f32[6,16,128]{2,1,0:T(8,128)S(1)}, u32[]{:S(2)}, u32[]{:S(2)}) collective-permute-start(f32[6,16,128]{2,1,0:T(8,128)S(1)} %get-tuple-element.5), channel_id=1, source_target_pairs={{0,1},{1,2},{2,3},{3,4},{4,5},{5,6},{6,7},{7,8},{8,9},{9,10},{10,1... | collective-permute-start | bytes 147464 | tf_op jit(solution)/shard_map/ppermute | solution.py:406

commit v3 on v2

--- a/solution.py
+++ b/solution.py
@@ -260,7 +260,7 @@
     orients = table_ref.shape[0] // 2
     reach = (taps_ref.shape[1] - 1) // 2
     span = 2 * reach
-    step = 4
+    step = max(d for d in range(1, 23) if out_ref.shape[0] % d == 0 and (d == 1 or d * planes <= 352))
 
     def lags_of(band, scale):
         return [
@@ -410,21 +410,48 @@
     return pieces, places
 
 
-def axial_matrices(axial_otf, planes):
+def axial_matrices(axial_otf, order):
+    planes = order.shape[0]
     wrapped = np.arange(planes)[:, None] * np.arange(planes)[None, :] % planes
     angle = wrapped * (2.0 * math.pi / planes)
     cosine = np.cos(angle).astype(np.float32)
     sine = np.sin(angle).astype(np.float32)
+    wrapped = order[:, None] * np.arange(planes, dtype=np.int32)[None, :] % planes
+    angle = wrapped.astype(jnp.float32) * (2.0 * math.pi / planes)
     real = axial_otf[:, 0, :, None]
     imag = axial_otf[:, 1, :, None]
     inner = jnp.concatenate(
         [real * cosine + imag * sine, real * sine - imag * cosine], axis=1
     )
-    both = np.concatenate([cosine, sine], axis=1) / planes
+    both = jnp.concatenate([jnp.cos(angle), jnp.sin(angle)], axis=1) * (1.0 / planes)
     return jnp.einsum(
         "zk,mkw->mzw", both, inner, precision=lax.Precision.HIGHEST,
         preferred_element_type=jnp.float32,
     )
+
+
+def by_permutes(ring):
+    return ring <= 16 and ring & (ring - 1) == 0 and ring > 2
+
+
+def exchange(sums):
+    ring = lax.axis_size("gz")
+    own = lax.axis_index("gz")
+    if not by_permutes(ring):
+        return lax.all_to_all(sums, "gz", 0, 0, tiled=True)
+    core, chip = own % 2, own // 2
+    paired = sums.reshape((ring // 2, 2) + sums.shape[1:])
+    mine = lax.dynamic_index_in_dim(paired, core, 1, keepdims=False)
+    other = lax.dynamic_index_in_dim(paired, 1 - core, 1, keepdims=False)
+    other = lax.ppermute(other, "gz", [(s, s ^ 1) for s in range(ring)])
+    both = jnp.stack([mine, other], axis=1)
+    parts = []
+    for bit in range(ring // 2):
+        part = lax.dynamic_index_in_dim(both, chip ^ bit, 0, keepdims=False)
+        if bit:
+            part = lax.ppermute(part, "gz", [(s, s ^ (2 * bit)) for s in range(ring)])
+        parts.append(part)
+    return jnp.concatenate(parts, axis=0)
 
 
 def shards(estimate, frames, phase_index, axial_otf, row_blur, column_taps):
@@ -436,8 +463,11 @@
     pad = -(-2 * span // 8) * 8
     table = jnp.asarray(pattern_table(orients, width * ring, row_count, pad))
     sums = data_sums(frames, phase_index, row_blur, column_taps, table, ring)
-    received = lax.all_to_all(sums, "gz", 0, 0, tiled=True)
-    forward = axial_matrices(axial_otf, planes)
+    received = exchange(sums)
+    order = jnp.arange(planes, dtype=jnp.int32)
+    if by_permutes(ring):
+        order = order ^ lax.axis_index("gz")
+    forward = axial_matrices(axial_otf, order)
     squared = jnp.einsum("mzw,mzv->mwv", forward, forward, precision=lax.Precision.HIGHEST)
     axial = exact_dot(squared.reshape(bands * planes, planes), estimate.reshape(planes, -1))
     axial = axial.reshape(bands, planes, width, row_count).transpose(0, 2, 1, 3)

time: 36.3 us -> 58.4 us (1.61)
  waiting for transfers between devices: 6.14 us -> 27.1 us
  Pallas kernels: 15.3 us -> 13.5 us
  starting transfers between devices: 12 us -> 13.4 us
  local copies, waits for them, and re-layouts: 1.28 us -> 2.55 us
    ppermute x0 -> x8, waiting for transfers between devices: none -> 27.1 us  [the longest x7 27.1 us: exchange(): part = lax.ppermute(part, 'gz', [(s, s ^ 2 * bit) for s in range(ring)])]
    ppermute x0 -> x8, starting transfers between devices: none -> 7.6 us  [the longest x7 7.04 us: exchange(): part = lax.ppermute(part, 'gz', [(s, s ^ 2 * bit) for s in range(ring)])]
    all_to_all x1 -> x0, starting transfers between devices: 7.56 us -> none  [shards(): received = lax.all_to_all(sums, 'gz', 0, 0, tiled=True)]
    ppermute x1, waiting for transfers between devices: 4.56 us -> 0.01 us  [spread(): lax.ppermute(piece, 'gz', [(s, (s + hop) % ring) for s in range(ring)])]
    pallas_call x1, Pallas kernels: 7.51 us -> 5.75 us  [estimate_part(): pl.pallas_call(estimate_kernel, out_shape=jax.ShapeDtypeStruct((width, pl...]
    ppermute x1, waiting for transfers between devices: 1.58 us -> 0.01 us  [spread(): lax.ppermute(piece, 'gz', [(s, (s - hop) % ring) for s in range(ring)])]
    ppermute x1, starting transfers between devices: 4.39 us -> 5.69 us  [spread(): lax.ppermute(piece, 'gz', [(s, (s - hop) % ring) for s in range(ring)])]
    squeeze x0 -> x1, local copies, waits for them, and re-layouts: none -> 1.22 us  [exchange(): other = lax.dynamic_index_in_dim(paired, 1 - core, 1, keepdims=False)]
  transfers between devices with their start and end apart: 3 -> 10, of which waited for: 2 -> 5; matrix products, arithmetic and copies ran while one was open for 7% -> 5% of each run, Pallas kernels for 21% -> 10%
where the time goes in v3:
time: 58.4 us; the launch traced here: 58.2 us
  waiting for transfers between devices  27.1 us (46%)
  Pallas kernels  13.5 us (23%)
  starting transfers between devices  13.4 us (23%)
  local copies, waits for them, and re-layouts  2.55 us (4%)
  matrix products  1.19 us (2%)
    ppermute x7, waiting for transfers between devices, exchange(): part = lax.ppermute(part, 'gz', [(s, s ^ 2 * bit) for s in range(ring)])  27.1 us
    ppermute x7, starting transfers between devices, exchange(): part = lax.ppermute(part, 'gz', [(s, s ^ 2 * bit) for s in range(ring)])  7.04 us
    pallas_call x1, Pallas kernels, data_sums(): pl.pallas_call(data_kernel, out_shape=jax.ShapeDtypeStruct((chunks, bands...  6.39 us
    pallas_call x1, Pallas kernels, estimate_part(): pl.pallas_call(estimate_kernel, out_shape=jax.ShapeDtypeStruct((width, pl...  5.75 us
    ppermute x1, starting transfers between devices, spread(): lax.ppermute(piece, 'gz', [(s, (s - hop) % ring) for s in range(ring)])  5.69 us
    pallas_call x1, Pallas kernels, combine(): pl.pallas_call(functools.partial(combine_kernel, places=places), out_shap...  1.38 us
    squeeze x1, local copies, waits for them, and re-layouts, exchange(): other = lax.dynamic_index_in_dim(paired, 1 - core, 1, keepdims=False)  1.22 us
  transfers between devices with their start and end apart: 10, of which 5 were waited for; matrix products, arithmetic and copies ran while one was open for 5% of the time, Pallas kernels for 10%

profile of v3, /device:TPU:0, one launch (start us, length us, event | category | flops | bytes accessed | tf_op | source)
XLA Modules:
  0.0 58.2 jit_solution(549024162169963114)
XLA Ops:
  0.0 0.0 copy-start.5
  0.0 0.0 copy-start.3
  0.0 0.0 copy-start.4
  0.0 6.4 %data_sums.1 = f32[16,3,32,128]{3,2,1,0:T(8,128)} custom-call(s32[3,5]{1,0:T(4,128)} %phase_hbm.1, f32[3,7]{1,0:T(4,128)} %taps_hbm.1, s32[3,5,1,512,128]{4,3,2,1,0:T(8,128)} %frames_hbm.1, f32[3,128,128]{2,1,0:T(8,128)} %blur_hbm.1, f32[6,544,128]{2,1,0:T(8,128)} %constant.99.clone.table_hbm), custom_call_target="tpu_custom_call" | custom-call | flops 872415232 | bytes 3932160 | tf_op jit(solution)/shard_map/data_sums/pallas_call | solution.py:231
  6.4 0.0 copy-start.2
  6.4 1.2 %dynamic-slice_bitcast_fusion = (f32[8,3,32,128]{3,2,1,0:T(8,128)S(1)}, f32[8,1,3,32,128]{4,3,2,1,0:T(8,128)S(1)}) fusion(f32[8,2,3,32,128]{4,3,2,1,0:T(8,128)} %bitcast.63, s32[]{:T(128)S(6)} %select_n.56, s32[]{:T(128)S(6)} %select_n.55), kind=kLoop, calls=%fused_computation.18 | loop fusion | bytes 1572872 | tf_op jit(solution)/shard_map/jit(dynamic_index_in_dim)/squeeze | solution.py:445
  7.6 0.6 collective-permute-start
  8.2 0.0 copy-done.5
  8.2 0.1 fusion.34
  8.4 0.0 copy-done.3
  8.4 0.0 copy-done.4
  8.4 0.2 fusion.18
  8.6 0.2 convolution_bitcast_fusion.1
  8.8 1.0 %constant_dynamic-slice_fusion.1.table_ref = f32[6,56,128]{2,1,0:T(8,128)S(1)} fusion(f32[6,544,128]{2,1,0:T(8,128)} %constant.99.clone.table_hbm, s32[]{:T(128)S(6)} %select_n.53), kind=kLoop, calls=%fused_computation.67 | loop fusion | bytes 344068 | tf_op jit(solution)/shard_map/dynamic_slice | solution.py:476
  9.8 0.0 copy-start
  9.8 0.0 copy-start.1
  9.8 0.0 copy-done.2
  9.8 0.8 %convolution_bitcast_fusion = f32[3,32,16,128]{3,2,1,0:T(8,128)S(1)} fusion(f32[3,16,16,1]{2,1,3,0:T(8,128)S(1)} %convolution_bitcast_fusion.1, f32[2,8,32,128]{3,2,1,0:T(8,128)S(1)} %bitcast.65), kind=kOutput, calls=%fused_computation.16 | convolution fusion | flops 37748736 | bytes 1051648 | tf_op jit(solution)/shard_map/dot_general | solution.py:20
  10.6 0.1 pad.4.axial_ref
  10.7 0.0 copy-done
  10.7 0.0 copy-done.1
  10.7 5.8 %estimate_part.1.estimate_ref = f32[44,16,128]{2,1,0:T(8,128)S(1)} custom-call(f32[3,7]{1,0:T(4,128)S(1)} %copy-done.1, f32[3,56,16,128]{3,2,1,0:T(8,128)S(1)} %pad.4.axial_ref, f32[6,56,128]{2,1,0:T(8,128)S(1)} %constant_dynamic-slice_fusion.1.table_ref, f32[3,128,128]{2,1,0:T(8,128)S(1)} %copy-done), custom_call_target="tpu_custom_call" | custom-call | flops 22145925120 | bytes 1376256 | tf_op jit(solution)/shard_map/estimate_part/pallas_call | solution.py:342
  16.5 0.1 collective-permute-start.9
  16.6 5.7 %collective-permute-start.8 = (f32[6,16,128]{2,1,0:T(8,128)S(1)}, f32[6,16,128]{2,1,0:T(8,128)S(1)}, u32[]{:S(2)}, u32[]{:S(2)}) collective-permute-start(f32[6,16,128]{2,1,0:T(8,128)S(1)} %get-tuple-element.14), channel_id=1, source_target_pairs={{0,15},{1,0},{2,1},{3,2},{4,3},{5,4},{6,5},{7,6},{8,7},{9,8},{10,9... | collective-permute-start | bytes 147464 | tf_op jit(solution)/shard_map/ppermute | solution.py:402
  22.3 0.1 copy.12
  22.4 0.1 copy.14.adjoint_ref
  22.5 0.0 collective-permute-done
  22.5 1.6 %collective-permute-start.6 = (f32[2,3,32,128]{3,2,1,0:T(8,128)S(1)}, f32[2,3,32,128]{3,2,1,0:T(8,128)S(1)}, u32[]{:S(2)}, u32[]{:S(2)}) collective-permute-start(f32[2,3,32,128]{3,2,1,0:T(8,128)S(1)} %fusion.17), channel_id=1, source_target_pairs={{0,12},{1,13},{2,14},{3,15},{4,8},{5,9},{6,10},{7,11},{8,4},{9,5},... | collective-permute-start | bytes 294920 | tf_op jit(solution)/shard_map/ppermute | solution.py:452
  24.2 0.3 collective-permute-start.7
  24.5 3.5 %collective-permute-start.1 = (f32[2,3,32,128]{3,2,1,0:T(8,128)S(1)}, f32[2,3,32,128]{3,2,1,0:T(8,128)S(1)}, u32[]{:S(2)}, u32[]{:S(2)}) collective-permute-start(f32[2,3,32,128]{3,2,1,0:T(8,128)S(1)} %get-tuple-element.6), channel_id=1, source_target_pairs={{0,2},{1,3},{2,0},{3,1},{4,6},{5,7},{6,4},{7,5},{8,10},{9,11},{10,... | collective-permute-start | bytes 294920 | tf_op jit(solution)/shard_map/ppermute | solution.py:452
  28.0 3.0 %collective-permute-done.1 = f32[2,3,32,128]{3,2,1,0:T(8,128)S(1)} collective-permute-done((f32[2,3,32,128]{3,2,1,0:T(8,128)S(1)}, f32[2,3,32,128]{3,2,1,0:T(8,128)S(1)}, u32[]{:S(2)}, u32[]{:S(2)}) %collective-permute-start.1) | collective-permute-done | bytes 98336 | tf_op jit(solution)/shard_map/ppermute | solution.py:452
  30.9 0.0 collective-permute-start.2
  30.9 5.4 %collective-permute-done.2 = f32[2,3,32,128]{3,2,1,0:T(8,128)S(1)} collective-permute-done((f32[2,3,32,128]{3,2,1,0:T(8,128)S(1)}, f32[2,3,32,128]{3,2,1,0:T(8,128)S(1)}, u32[]{:S(2)}, u32[]{:S(2)}) %collective-permute-start.2) | collective-permute-done | bytes 98336 | tf_op jit(solution)/shard_map/ppermute | solution.py:452
  36.4 1.1 %collective-permute-start.3 = (f32[2,3,32,128]{3,2,1,0:T(8,128)S(1)}, f32[2,3,32,128]{3,2,1,0:T(8,128)S(1)}, u32[]{:S(2)}, u32[]{:S(2)}) collective-permute-start(f32[2,3,32,128]{3,2,1,0:T(8,128)S(1)} %get-tuple-element.8), channel_id=1, source_target_pairs={{0,6},{1,7},{2,4},{3,5},{4,2},{5,3},{6,0},{7,1},{8,14},{9,15},{10,... | collective-permute-start | bytes 294920 | tf_op jit(solution)/shard_map/ppermute | solution.py:452
  37.5 5.4 %collective-permute-done.3 = f32[2,3,32,128]{3,2,1,0:T(8,128)S(1)} collective-permute-done((f32[2,3,32,128]{3,2,1,0:T(8,128)S(1)}, f32[2,3,32,128]{3,2,1,0:T(8,128)S(1)}, u32[]{:S(2)}, u32[]{:S(2)}) %collective-permute-start.3) | collective-permute-done | bytes 98336 | tf_op jit(solution)/shard_map/ppermute | solution.py:452
  42.9 0.4 collective-permute-start.4
  43.3 6.7 %collective-permute-done.4 = f32[2,3,32,128]{3,2,1,0:T(8,128)S(1)} collective-permute-done((f32[2,3,32,128]{3,2,1,0:T(8,128)S(1)}, f32[2,3,32,128]{3,2,1,0:T(8,128)S(1)}, u32[]{:S(2)}, u32[]{:S(2)}) %collective-permute-start.4) | collective-permute-done | bytes 98336 | tf_op jit(solution)/shard_map/ppermute | solution.py:452
  50.1 0.1 collective-permute-start.5
  50.2 6.5 %collective-permute-done.5 = f32[2,3,32,128]{3,2,1,0:T(8,128)S(1)} collective-permute-done((f32[2,3,32,128]{3,2,1,0:T(8,128)S(1)}, f32[2,3,32,128]{3,2,1,0:T(8,128)S(1)}, u32[]{:S(2)}, u32[]{:S(2)}) %collective-permute-start.5) | collective-permute-done | bytes 98336 | tf_op jit(solution)/shard_map/ppermute | solution.py:452
  56.8 0.0 collective-permute-done.6
  56.8 0.0 collective-permute-done.7
  56.8 0.0 collective-permute-done.9.refs_1_
  56.8 0.0 collective-permute-done.8.refs_0_
  56.8 1.4 %combine.1 = f32[512,128]{1,0:T(8,128)} custom-call(f32[16,48]{1,0:T(8,128)S(1)} %copy.14.adjoint_ref, f32[44,16,128]{2,1,0:T(8,128)S(1)} %estimate_part.1.estimate_ref, f32[1536,128]{1,0:T(8,128)S(1)} %bitcast.59, f32[6,16,128]{2,1,0:T(8,128)S(1)} %collective-permute-done.8.refs_0_, f32[6,16,128]{2,1,0:T(8,128)S(1)} %collective-permute-done.9.refs_1_), custom_call_target="tpu_custom_call" | custom-call | flops 6291456 | bytes 786432 | tf_op jit(solution)/shard_map/combine/pallas_call | solution.py:379
  (16 shorter events, 0.2 us)
Async XLA Ops:
  0.0 8.2 %copy-start.5 = (f32[3,2,16]{2,1,0:T(2,128)S(1)}, f32[3,2,16]{2,1,0:T(2,128)}, u32[]{:S(2)}) copy-start(f32[3,2,16]{2,1,0:T(2,128)} %param.13) | copy-start | bytes 1156
  0.0 8.4 %copy-start.3 = (f32[16,16]{0,1:T(8,128)S(1)}, f32[16,16]{0,1:T(8,128)}, u32[]{:S(2)}) copy-start(f32[16,16]{0,1:T(8,128)} %constant.102.clone) | copy-start | bytes 3076
  0.0 8.4 %copy-start.4 = (f32[16,16]{0,1:T(8,128)S(1)}, f32[16,16]{0,1:T(8,128)}, u32[]{:S(2)}) copy-start(f32[16,16]{0,1:T(8,128)} %constant.101.clone) | copy-start | bytes 3076
  6.4 3.4 %copy-start.2 = (f32[16,32,128]{2,1,0:T(8,128)S(1)}, f32[16,32,128]{2,1,0:T(8,128)}, u32[]{:S(2)}) copy-start(f32[16,32,128]{2,1,0:T(8,128)} %param.10) | copy-start | bytes 786436
  7.6 14.8 %collective-permute-start = (f32[8,3,32,128]{3,2,1,0:T(8,128)S(1)}, f32[8,3,32,128]{3,2,1,0:T(8,128)S(1)}, u32[]{:S(2)}, u32[]{:S(2)}) collective-permute-start(f32[8,3,32,128]{3,2,1,0:T(8,128)S(1)} %get-tuple-element.11), channel_id=1, source_target_pairs={{0,1},{1,0},{2,3},{3,2},{4,5},{5,4},{6,7},{7,6},{8,9},{9,8},{10,11... | collective-permute-start | bytes 1179656 | tf_op jit(solution)/shard_map/ppermute | solution.py:446
  9.8 1.0 %copy-start = (f32[3,128,128]{2,1,0:T(8,128)S(1)}, f32[3,128,128]{2,1,0:T(8,128)}, u32[]{:S(2)}) copy-start(f32[3,128,128]{2,1,0:T(8,128)} %blur_hbm.1) | copy-start | bytes 589828
  9.8 1.0 %copy-start.1 = (f32[3,7]{1,0:T(4,128)S(1)}, f32[3,7]{1,0:T(4,128)}, u32[]{:S(2)}) copy-start(f32[3,7]{1,0:T(4,128)} %taps_hbm.1) | copy-start | bytes 256
  16.5 40.3 %collective-permute-start.9 = (f32[6,16,128]{2,1,0:T(8,128)S(1)}, f32[6,16,128]{2,1,0:T(8,128)S(1)}, u32[]{:S(2)}, u32[]{:S(2)}) collective-permute-start(f32[6,16,128]{2,1,0:T(8,128)S(1)} %get-tuple-element.13), channel_id=1, source_target_pairs={{0,1},{1,2},{2,3},{3,4},{4,5},{5,6},{6,7},{7,8},{8,9},{9,10},{10,1... | collective-permute-start | bytes 147464 | tf_op jit(solution)/shard_map/ppermute | solution.py:406
  16.6 40.2 %collective-permute-start.8 = (f32[6,16,128]{2,1,0:T(8,128)S(1)}, f32[6,16,128]{2,1,0:T(8,128)S(1)}, u32[]{:S(2)}, u32[]{:S(2)}) collective-permute-start(f32[6,16,128]{2,1,0:T(8,128)S(1)} %get-tuple-element.14), channel_id=1, source_target_pairs={{0,15},{1,0},{2,1},{3,2},{4,3},{5,4},{6,5},{7,6},{8,7},{9,8},{10,9... | collective-permute-start | bytes 147464 | tf_op jit(solution)/shard_map/ppermute | solution.py:402
  22.5 34.3 %collective-permute-start.6 = (f32[2,3,32,128]{3,2,1,0:T(8,128)S(1)}, f32[2,3,32,128]{3,2,1,0:T(8,128)S(1)}, u32[]{:S(2)}, u32[]{:S(2)}) collective-permute-start(f32[2,3,32,128]{3,2,1,0:T(8,128)S(1)} %fusion.17), channel_id=1, source_target_pairs={{0,12},{1,13},{2,14},{3,15},{4,8},{5,9},{6,10},{7,11},{8,4},{9,5},... | collective-permute-start | bytes 294920 | tf_op jit(solution)/shard_map/ppermute | solution.py:452
  24.2 32.6 %collective-permute-start.7 = (f32[2,3,32,128]{3,2,1,0:T(8,128)S(1)}, f32[2,3,32,128]{3,2,1,0:T(8,128)S(1)}, u32[]{:S(2)}, u32[]{:S(2)}) collective-permute-start(f32[2,3,32,128]{3,2,1,0:T(8,128)S(1)} %get-tuple-element.5), channel_id=1, source_target_pairs={{0,14},{1,15},{2,12},{3,13},{4,10},{5,11},{6,8},{7,9},{8,6},{9,7},... | collective-permute-start | bytes 294920 | tf_op jit(solution)/shard_map/ppermute | solution.py:452
  24.5 6.4 %collective-permute-start.1 = (f32[2,3,32,128]{3,2,1,0:T(8,128)S(1)}, f32[2,3,32,128]{3,2,1,0:T(8,128)S(1)}, u32[]{:S(2)}, u32[]{:S(2)}) collective-permute-start(f32[2,3,32,128]{3,2,1,0:T(8,128)S(1)} %get-tuple-element.6), channel_id=1, source_target_pairs={{0,2},{1,3},{2,0},{3,1},{4,6},{5,7},{6,4},{7,5},{8,10},{9,11},{10,... | collective-permute-start | bytes 294920 | tf_op jit(solution)/shard_map/ppermute | solution.py:452
  30.9 5.4 %collective-permute-start.2 = (f32[2,3,32,128]{3,2,1,0:T(8,128)S(1)}, f32[2,3,32,128]{3,2,1,0:T(8,128)S(1)}, u32[]{:S(2)}, u32[]{:S(2)}) collective-permute-start(f32[2,3,32,128]{3,2,1,0:T(8,128)S(1)} %get-tuple-element.7), channel_id=1, source_target_pairs={{0,4},{1,5},{2,6},{3,7},{4,0},{5,1},{6,2},{7,3},{8,12},{9,13},{10,... | collective-permute-start | bytes 294920 | tf_op jit(solution)/shard_map/ppermute | solution.py:452
  36.4 6.6 %collective-permute-start.3 = (f32[2,3,32,128]{3,2,1,0:T(8,128)S(1)}, f32[2,3,32,128]{3,2,1,0:T(8,128)S(1)}, u32[]{:S(2)}, u32[]{:S(2)}) collective-permute-start(f32[2,3,32,128]{3,2,1,0:T(8,128)S(1)} %get-tuple-element.8), channel_id=1, source_target_pairs={{0,6},{1,7},{2,4},{3,5},{4,2},{5,3},{6,0},{7,1},{8,14},{9,15},{10,... | collective-permute-start | bytes 294920 | tf_op jit(solution)/shard_map/ppermute | solution.py:452
  42.9 7.1 %collective-permute-start.4 = (f32[2,3,32,128]{3,2,1,0:T(8,128)S(1)}, f32[2,3,32,128]{3,2,1,0:T(8,128)S(1)}, u32[]{:S(2)}, u32[]{:S(2)}) collective-permute-start(f32[2,3,32,128]{3,2,1,0:T(8,128)S(1)} %get-tuple-element.9), channel_id=1, source_target_pairs={{0,8},{1,9},{2,10},{3,11},{4,12},{5,13},{6,14},{7,15},{8,0},{9,1},... | collective-permute-start | bytes 294920 | tf_op jit(solution)/shard_map/ppermute | solution.py:452
  50.1 6.7 %collective-permute-start.5 = (f32[2,3,32,128]{3,2,1,0:T(8,128)S(1)}, f32[2,3,32,128]{3,2,1,0:T(8,128)S(1)}, u32[]{:S(2)}, u32[]{:S(2)}) collective-permute-start(f32[2,3,32,128]{3,2,1,0:T(8,128)S(1)} %get-tuple-element.10), channel_id=1, source_target_pairs={{0,10},{1,11},{2,8},{3,9},{4,14},{5,15},{6,12},{7,13},{8,2},{9,3},... | collective-permute-start | bytes 294920 | tf_op jit(solution)/shard_map/ppermute | solution.py:452
